TPU v7x, 32 devices: a whole 2x2x4 slice. The times are simulated.
32 devices in a mesh: dp: 8 (over z, y), tp: 4 (over x, core).
Axes of the slice: x: 2, y: 2, z: 4, core: 2. Of those that a mesh axis runs over, the one named last changes fastest.
Arguments:
- hidden: bfloat16 [16, 4096], P('dp'), may hold values from -6 to 6
- attention_norm_gain: bfloat16 [4096], replicated, may hold values from 0.5 to 1.5
- query_key_value_weight: bfloat16 [4096, 4, 1280], P('dp', 'tp'), may hold values from -0.09375 to 0.09375
- key_value_cache: bfloat16 [16, 2048, 4, 256], P('dp', None, 'tp'), may hold values from -6 to 6
- cache_fill_lengths: int32 [16], P('dp'), may hold values from 2 to 2048
- output_weight_frozen: bfloat16 [4, 1024, 4096], P('tp', None, 'dp'), may hold values from -0.09375 to 0.09375
- adapter_down_transposed: bfloat16 [64, 4, 1024], P(None, 'tp', 'dp'), may hold values from -0.09375 to 0.09375
- adapter_up_matrix: bfloat16 [64, 4, 1024], P(None, 'tp', 'dp'), may hold values from -0.75 to 0.75
- attention_rows: bfloat16 [4096, 4096], P('dp', 'tp'), may hold values from -6 to 6
- upstream: bfloat16 [4096, 4096], P('dp', 'tp'), may hold values from -6 to 6
- rewards: float32 [16], P('dp'), may hold values from 0 to 2
- prompt_group_index: int32 [16], P('dp'), may hold values from 0 to 3, as said below
- completion_live_lengths: int32 [16], P('dp'), may hold values from 1 to 256
Outputs:
- decoded: float32 [16, 4096], P('dp')
- adapted_output_rows: float32 [4096, 4096], P('dp', 'tp')
- grad_lora_a_t: float32 [64, 4, 1024], P(None, 'tp', 'dp')
- grad_lora_b: float32 [64, 4, 1024], P(None, 'tp', 'dp')
Inputs may be any that keep to these rules, and one draw needn't show every extreme that they name: `prompt_group_index`: each prompt holds exactly 4 rollouts.
All inputs are finite; a program needn't handle non-finite values.
Results may differ from a plain program's by a relative error of at most 0.0041.
Values may be sent and summed in bfloat16 or wider, within the bound.
A program may use at most 128 MiB of HBM per device.

v0:
```python
import math

import jax
import jax.numpy as jnp
from jax import lax
from jax.experimental import pallas as pl
from jax.experimental.pallas import tpu as pltpu
from jax.sharding import PartitionSpec as P

HD = 128
HEADS_TP = 8
GROUP = 4
COMP = 256


adapter_scale = 2.0


def rms_norm(decode_state, gain):
    scale = lax.rsqrt(jnp.mean(decode_state * decode_state, axis=-1, keepdims=True) + 1e-05)
    return decode_state * scale * gain.astype(jnp.float32)


def attend(query, cache, lengths, new_keys, new_values):
    head = query.shape[-1]
    slots = cache.shape[1]
    factor = 1.0 / math.sqrt(head)
    keys = cache[:, :, :head].astype(jnp.float32)
    values = cache[:, :, head:]
    scores = jnp.einsum("bhd,bcd->bhc", query, keys, precision=lax.Precision.HIGHEST) * factor
    valid = jnp.arange(slots, dtype=jnp.int32)[None, None, :] < lengths[:, None, None]
    scores = jnp.where(valid, scores, -1e30)
    extra = jnp.einsum("bhd,bed->bhe", query, new_keys, precision=lax.Precision.HIGHEST) * factor
    joined = jnp.concatenate([scores, extra], axis=-1)
    top = jnp.max(joined, axis=-1, keepdims=True)
    expo = jnp.exp(joined - top)
    probs = (expo / jnp.sum(expo, axis=-1, keepdims=True)).astype(jnp.bfloat16)
    out = jnp.einsum("bhc,bcd->bhd", probs[..., :slots], values, preferred_element_type=jnp.float32)
    out = out + jnp.einsum(
        "bhe,bed->bhd",
        probs[..., slots:].astype(jnp.float32),
        new_values,
        precision=lax.Precision.HIGHEST,
    )
    return out.astype(jnp.bfloat16).reshape(query.shape[0], -1)


MESH = pl.DeviceIdType.MESH
F32 = jnp.float32
BF16 = jnp.bfloat16
NT = (((1,), (1,)), ((), ()))
TN = (((0,), (0,)), ((), ()))
CHUNK = 256
LINE_PARTS = 8
ROW_PARTS = 8


def split3(v):
    hi = v.astype(BF16)
    rest = v - hi.astype(F32)
    mid = rest.astype(BF16)
    lo = (rest - mid.astype(F32)).astype(BF16)
    return jnp.concatenate([hi, mid, lo], axis=0)


def exact_dot(v, w, dims=(((1,), (0,)), ((), ()))):
    n = v.shape[0]
    r = lax.dot_general(split3(v), w, dims, preferred_element_type=F32)
    return r[:n] + r[n : 2 * n] + r[2 * n :]


def rows_of(ref, n):
    return jnp.concatenate([ref[i] for i in range(n)], axis=0)


def lanes_of(ref, n):
    return jnp.concatenate([ref[i] for i in range(n)], axis=1)


def fused_kernel(
    ndp,
    ntp,
    h_ref,
    gain_ref,
    wqkv_ref,
    cache_ref,
    lens_ref,
    wo_ref,
    a_ref,
    b_ref,
    x_ref,
    up_ref,
    rew_ref,
    idx_ref,
    live_ref,
    dec_ref,
    out_ref,
    ga_ref,
    gb_ref,
    hsend,
    stats_ref,
    hbuf,
    abuf,
    bbuf,
    bdbuf,
    statbuf,
    qsend,
    qrecv,
    asend,
    arecv,
    usend,
    urecv,
    fsend,
    frecv,
    lbsend,
    lbrecv,
    gsend,
    grecv,
    wt_ref,
    xbuf,
    wbuf,
    pbuf,
    prcv,
    ds_s,
    ds_r,
    ts_s,
    ts_r,
    bd_s,
    bd_r,
    xs_s,
    xs_r,
    wl_s,
    wl_r,
    ps_s,
    ps_r,
):
    d = lax.axis_index("dp")
    t = lax.axis_index("tp")
    z, y = d // 2, d % 2
    x, c = t // 2, t % 2
    nz = ndp // 2
    rolls, model = h_ref.shape
    width = model // ndp
    rank = a_ref.shape[0]
    piece = a_ref.shape[1]
    chunks = wo_ref.shape[1] // CHUNK
    qkvw = wqkv_ref.shape[1]
    rows = x_ref.shape[0]

    barrier = pltpu.get_barrier_semaphore()
    for i in range(ndp):
        for j in range(ntp):
            if i or j:
                pl.semaphore_signal(
                    barrier,
                    inc=1,
                    device_id=((d + i) % ndp, (t + j) % ntp),
                    device_id_type=MESH,
                )
    pl.semaphore_wait(barrier, ndp * ntp - 1)

    sent = []

    def send(src, dst, s, r, dev):
        cp = pltpu.make_async_remote_copy(
            src_ref=src, dst_ref=dst, send_sem=s, recv_sem=r, device_id=dev, device_id_type=MESH
        )
        return cp

    def dp_start(e, src, dst):
        for off in range(1, ndp):
            peer = (d + off) % ndp
            cp = send(src(peer), dst.at[d], ds_s.at[e, off], ds_r.at[e, off], (peer, t))
            cp.start()
            sent.append(cp)

    def dp_wait(e, src, dst):
        for off in range(1, ndp):
            frm = (d + ndp - off) % ndp
            send(src(d), dst.at[frm], ds_s.at[e, off], ds_r.at[e, off], (frm, t)).wait_recv()

    def tp_start(e, src, dst):
        for off in range(1, ntp):
            peer = (t + off) % ntp
            cp = send(src, dst.at[t], ts_s.at[e, off], ts_r.at[e, off], (d, peer))
            cp.start()
            sent.append(cp)

    def tp_wait(e, src, dst):
        for off in range(1, ntp):
            frm = (t + ntp - off) % ntp
            send(src, dst.at[frm], ts_s.at[e, off], ts_r.at[e, off], (d, frm)).wait_recv()

    hidden = h_ref[...].astype(F32)
    for i in range(ndp):
        hsend[i] = hidden[:, i * width : (i + 1) * width]
    lane = lax.broadcasted_iota(jnp.int32, (1, 128), 1)
    ones = [jnp.where(lane == idx_ref[r], 1.0, 0.0) for r in range(rolls)]
    stats_ref[...] = jnp.zeros_like(stats_ref)
    for r in range(rolls):
        stats_ref[0:1] += ones[r] * rew_ref[r]
        stats_ref[1:2] += ones[r] * (rew_ref[r] * rew_ref[r])

    dp_start(0, lambda p: hsend.at[p], hbuf)
    hbuf[d] = hsend[d]
    dp_start(1, lambda p: a_ref, abuf)
    abuf[d] = a_ref[...]
    dp_start(2, lambda p: b_ref, bbuf)
    bbuf[d] = b_ref[...]
    dp_start(3, lambda p: stats_ref, statbuf)
    statbuf[d] = stats_ref[...]
    per = width // piece
    half = ndp // per
    bdst = t * half + d // per
    bslot = d % per
    for j in range(ntp):
        tj = (t + j) % ntp
        if j == 0:
            here = bdst == d

            @pl.when(here)
            def _():
                bdbuf[bslot] = b_ref[...]

            @pl.when(jnp.logical_not(here))
            def _():
                send(b_ref, bdbuf.at[bslot], bd_s.at[0], bd_r.at[bslot], (bdst, tj)).start()

        else:
            cp = send(b_ref, bdbuf.at[bslot], bd_s.at[j], bd_r.at[bslot], (bdst, tj))
            cp.start()
            sent.append(cp)
    mate = 2 * x + (1 - c)
    other_y = 2 * z + (1 - y)
    xcp = send(x_ref, xbuf.at[y, c], xs_s.at[0], xs_r.at[0], (d, mate))
    xcp.start()
    sent.append(xcp)
    xbuf[y, c] = x_ref[...]

    def row_send(k):
        part = rows // ROW_PARTS
        seg = pl.ds(k * part, part)
        send(
            x_ref.at[seg], xbuf.at[y, c, seg], xs_s.at[1], xs_r.at[1], (other_y, t)
        ).start()

    def rows_whole():
        return send(x_ref, xbuf.at[1 - y, c], xs_s.at[1], xs_r.at[1], (other_y, t))

    def relay(dst_core):
        return send(
            xbuf.at[1 - y, c], xbuf.at[1 - y, dst_core], xs_s.at[2], xs_r.at[2], (d, mate)
        )

    def line(ch, off, seg):
        zt = (z + off) % nz
        cols = pl.ds(ch * CHUNK, CHUNK)
        return send(
            wo_ref.at[seg, cols],
            wbuf.at[z // 2, c, ch, seg],
            wl_s.at[ch, off],
            wl_r.at[z // 2, c, ch],
            (2 * zt + y, 2 * x + z % 2),
        )

    def quantum(k):
        ch, part = k // LINE_PARTS, k % LINE_PARTS
        size = wo_ref.shape[0] // LINE_PARTS
        seg = pl.ds(part * size, size)
        for off in (1, 3, 2):
            line(ch, off, seg).start()

        @pl.when(z % 2 != c)
        def _():
            line(ch, 0, seg).start()

    pending = list(range(chunks * LINE_PARTS))
    row_parts = list(range(ROW_PARTS))

    def bulk(n, m=0):
        for _ in range(min(n, len(pending))):
            quantum(pending.pop(0))
        for _ in range(min(m, len(row_parts))):
            row_send(row_parts.pop(0))

    bulk(1, 1)

    @pl.when(z % 2 == c)
    def _():
        for ch in range(chunks):
            wbuf[z // 2, c, ch] = wo_ref[:, ch * CHUNK : (ch + 1) * CHUNK]

    dp_wait(0, lambda p: hsend.at[p], hbuf)
    state = rows_of(hbuf, ndp)
    gain = gain_ref[:, pl.ds(pl.multiple_of(d * width, width), width)].astype(F32)
    new_k, new_v = [], []
    factor = 1.0 / math.sqrt(HD)

    for step in range(2):
        squares = jnp.sum(state * state, axis=-1, keepdims=True)
        part = exact_dot(state * gain, wqkv_ref[...])
        both = jnp.concatenate([part, jnp.broadcast_to(squares, (ndp * rolls, 128))], axis=1)
        for i in range(ndp):
            qsend[step, i] = both[i * rolls : (i + 1) * rolls]
        dp_start(4 + 2 * step, lambda p: qsend.at[step, p], qrecv.at[step])
        bulk(1, 2)
        qrecv[step, d] = qsend[step, d]
        if step == 0:
            dp_wait(1, lambda p: a_ref, abuf)
            at = lanes_of(abuf, ndp)
            dp_wait(2, lambda p: b_ref, bbuf)
            bt = lanes_of(bbuf, ndp)
            dp_wait(3, lambda p: stats_ref, statbuf)
            tot = statbuf[0]
            for i in range(1, ndp):
                tot = tot + statbuf[i]
            mean = tot[0:1] / GROUP
            std = jnp.sqrt(jnp.maximum(tot[1:2] / GROUP - mean * mean, 0.09))
            for r in range(rolls):
                one, rew = ones[r], rew_ref[r]
                live = live_ref[r].astype(F32)
                adv = (rew - jnp.sum(one * mean, axis=1, keepdims=True)) / jnp.sum(
                    one * std, axis=1, keepdims=True
                )
                slot = lax.broadcasted_iota(jnp.int32, (COMP, 1), 0).astype(F32)
                row_w = jnp.where(slot < live, adv / live, 0.0)
                seg = pl.ds(r * COMP, COMP)
                wt_ref[seg, :] = (row_w * up_ref[seg, :].astype(F32)).astype(BF16)
            lbsend[0] = lax.dot_general(at, x_ref[...], NT, preferred_element_type=F32)
            lbsend[1] = lax.dot_general(bt, wt_ref[...], NT, preferred_element_type=F32)
        dp_wait(4 + 2 * step, lambda p: qsend.at[step, p], qrecv.at[step])
        total = qrecv[step, 0]
        for i in range(1, ndp):
            total = total + qrecv[step, i]
        qkv = total[:, :qkvw] * lax.rsqrt(total[:, qkvw : qkvw + 1] / model + 1e-05)
        new_k.append(qkv[:, HEADS_TP * HD : HEADS_TP * HD + HD])
        new_v.append(qkv[:, HEADS_TP * HD + HD :])
        for b in range(rolls):
            q = jnp.concatenate(
                [qkv[b : b + 1, h * HD : (h + 1) * HD] for h in range(HEADS_TP)], axis=0
            )
            scores = exact_dot(q, cache_ref[b, :, :HD], NT) * factor
            pos = lax.broadcasted_iota(jnp.int32, scores.shape, 1)
            scores = jnp.where(pos < lens_ref[b], scores, -1e30)
            extra = [
                jnp.sum(q * k[b : b + 1], axis=-1, keepdims=True) * factor for k in new_k
            ]
            top = jnp.max(scores, axis=-1, keepdims=True)
            for e in extra:
                top = jnp.maximum(top, e)
            expo = jnp.exp(scores - top)
            ee = [jnp.exp(e - top) for e in extra]
            den = jnp.sum(expo, axis=-1, keepdims=True)
            for e in ee:
                den = den + e
            att = jnp.dot(
                (expo / den).astype(BF16), cache_ref[b, :, HD:], preferred_element_type=F32
            )
            for e, v in zip(ee, new_v):
                att = att + (e / den).astype(BF16).astype(F32) * v[b : b + 1]
            att = att.astype(BF16).astype(F32)
            asend[step, b : b + 1, :] = jnp.concatenate(
                [att[h : h + 1] for h in range(HEADS_TP)], axis=1
            )
        dp_start(5 + 2 * step, lambda p: asend.at[step], arecv.at[step])
        bulk(1, 1)
        arecv[step, d] = asend[step]
        if step == 0:
            tp_start(2, lbsend, lbrecv)
            lbrecv[t] = lbsend[...]
        else:
            tp_wait(2, lbsend, lbrecv)
            lb = lbrecv[0]
            for i in range(1, ntp):
                lb = lb + lbrecv[i]
            lb = lb.astype(BF16)
            low_t, back_t = lb[0], lb[1]
            ga = adapter_scale * jnp.dot(back_t, x_ref[...], preferred_element_type=F32)
            gb = adapter_scale * jnp.dot(low_t, wt_ref[...], preferred_element_type=F32)
            for i in range(ndp):
                gsend[i, 0] = ga[:, i * piece : (i + 1) * piece]
                gsend[i, 1] = gb[:, i * piece : (i + 1) * piece]
        dp_wait(5 + 2 * step, lambda p: asend.at[step], arecv.at[step])
        attended = rows_of(arecv.at[step], ndp).astype(BF16)
        usend[step, :, :width] = jnp.dot(attended, wo_ref[...], preferred_element_type=F32)
        usend[step, :, width:] = jnp.concatenate(
            [
                lax.dot_general(attended, at, NT, preferred_element_type=F32),
                jnp.zeros((ndp * rolls, 128 - rank), F32),
            ],
            axis=1,
        )
        tp_start(step, usend.at[step], urecv.at[step])
        bulk(1, 1)
        urecv[step, t] = usend[step]
        if step == 0:
            src_t = d // half
            for j in range(per):
                frm = (d % half) * per + j
                same = jnp.logical_and(src_t == t, frm == d)

                @pl.when(jnp.logical_not(same))
                def _():
                    send(b_ref, bdbuf.at[j], bd_s.at[0], bd_r.at[j], (frm, src_t)).wait_recv()

            bd = lanes_of(bdbuf, per)
        tp_wait(step, usend.at[step], urecv.at[step])
        upd = urecv[step, 0]
        for i in range(1, ntp):
            upd = upd + urecv[step, i]
        state = state + (
            upd[:, :width] + adapter_scale * exact_dot(upd[:, width : width + rank], bd)
        )

    for i in range(ndp):
        fsend[i] = state[i * rolls : (i + 1) * rolls]
    dp_start(8, lambda p: fsend.at[p], frecv)
    frecv[d] = fsend[d]
    dp_start(9, lambda p: gsend.at[p], grecv)
    grecv[d] = gsend[d]
    bulk(len(pending), len(row_parts))
    rows_whole().wait_recv()
    relay(c).start()
    out_ref[...] = adapter_scale * lax.dot_general(low_t, bt, TN, preferred_element_type=F32)
    send(x_ref, xbuf.at[y, 1 - c], xs_s.at[0], xs_r.at[0], (d, mate)).wait_recv()
    dp_wait(8, lambda p: fsend.at[p], frecv)
    for i in range(ndp):
        dec_ref[:, i * width : (i + 1) * width] = frecv[i]
    relay(1 - c).wait_recv()

    def share(dx, dy, ch):
        zz = jnp.where(dx == 1, 1 - x, x)
        yy = jnp.where(dy == 1, 1 - y, y)
        return send(
            pbuf.at[dx, dy, ch],
            prcv.at[dx, dy, ch],
            ps_s.at[dx, dy, ch],
            ps_r.at[dx, dy, ch],
            (2 * z + yy, 2 * zz + c),
        )

    def stage(q, _):
        ch, r = q // 4, q % 4
        dx, dy = 1 - r // 2, 1 - r % 2
        zz = jnp.where(dx == 1, 1 - x, x)
        yy = jnp.where(dy == 1, 1 - y, y)

        @pl.when(dy == 1)
        def _():
            for cc in range(2):
                mine = jnp.logical_and(c + 2 * zz == z, c == cc)

                @pl.when(jnp.logical_not(mine))
                def _():
                    send(
                        wo_ref.at[:, pl.ds(0, CHUNK)],
                        wbuf.at[zz, cc, ch],
                        wl_s.at[0, 0],
                        wl_r.at[zz, cc, ch],
                        (d, mate),
                    ).wait_recv()

        p = jnp.dot(xbuf[yy, 0], wbuf[zz, 0, ch], preferred_element_type=F32)
        p = p + jnp.dot(xbuf[yy, 1], wbuf[zz, 1, ch], preferred_element_type=F32)
        last = r == 3

        @pl.when(jnp.logical_not(last))
        def _():
            pbuf[dx, dy, ch] = p
            share(dx, dy, ch).start()

        @pl.when(last)
        def _():
            cols = pl.ds(pl.multiple_of((y * chunks + ch) * CHUNK, CHUNK), CHUNK)
            out_ref[:, cols] += p

        return 0

    lax.fori_loop(0, 4 * chunks, stage, 0)

    dp_wait(9, lambda p: gsend.at[p], grecv)
    g = grecv[0]
    for i in range(1, ndp):
        g = g + grecv[i]
    ga_ref[...] = g[0]
    gb_ref[...] = g[1]
    for ch in range(chunks):
        for dx, dy in ((1, 0), (0, 1), (1, 1)):
            share(dx, dy, ch).wait_recv()
            yy = (y + dy) % 2
            cols = pl.ds(pl.multiple_of((yy * chunks + ch) * CHUNK, CHUNK), CHUNK)
            out_ref[:, cols] += prcv[dx, dy, ch]

    whole = pl.ds(0, wo_ref.shape[0])
    for ch in range(chunks):
        for off in range(1, nz):
            line(ch, off, whole).wait_send()

        @pl.when(z % 2 != c)
        def _():
            line(ch, 0, whole).wait_send()

        for dx, dy in ((1, 0), (0, 1), (1, 1)):
            share(dx, dy, ch).wait_send()
    rows_whole().wait_send()
    relay(c).wait_send()

    @pl.when(bdst != d)
    def _():
        send(b_ref, bdbuf.at[bslot], bd_s.at[0], bd_r.at[bslot], (bdst, t)).wait_send()

    for cp in sent:
        cp.wait_send()


def fused_shards(
    ndp,
    ntp,
    hidden,
    attention_norm_gain,
    query_key_value_weight,
    key_value_cache,
    cache_fill_lengths,
    output_weight_frozen,
    adapter_down_transposed,
    adapter_up_matrix,
    attention_rows,
    upstream,
    rewards,
    prompt_group_index,
    completion_live_lengths,
):
    rolls, model = hidden.shape
    width = model // ndp
    rank, _, piece = adapter_down_transposed.shape
    rows, shard = attention_rows.shape
    qkvw = query_key_value_weight.shape[2]
    feats = output_weight_frozen.shape[1]
    chunks = width // CHUNK
    vm = pl.BlockSpec(memory_space=pltpu.VMEM)
    sm = pl.BlockSpec(memory_space=pltpu.SMEM)
    dma = pltpu.SemaphoreType.DMA
    V = pltpu.VMEM
    dec, out, ga, gb = pl.pallas_call(
        lambda *refs: fused_kernel(ndp, ntp, *refs),
        out_shape=(
            jax.ShapeDtypeStruct((rolls, model), F32),
            jax.ShapeDtypeStruct((rows, shard), F32),
            jax.ShapeDtypeStruct((rank, piece), F32),
            jax.ShapeDtypeStruct((rank, piece), F32),
        ),
        in_specs=[vm, vm, vm, vm, sm, vm, vm, vm, vm, vm, sm, sm, sm],
        out_specs=(vm, vm, vm, vm),
        scratch_shapes=[
            V((ndp, rolls, width), F32),
            V((8, 128), F32),
            V((ndp, rolls, width), F32),
            V((ndp, rank, piece), BF16),
            V((ndp, rank, piece), BF16),
            V((width // piece, rank, piece), BF16),
            V((ndp, 8, 128), F32),
            V((2, ndp, rolls, qkvw + 128), F32),
            V((2, ndp, rolls, qkvw + 128), F32),
            V((2, rolls, feats), F32),
            V((2, ndp, rolls, feats), F32),
            V((2, ndp * rolls, width + 128), F32),
            V((2, ntp, ndp * rolls, width + 128), F32),
            V((ndp, rolls, width), F32),
            V((ndp, rolls, width), F32),
            V((2, rank, rows), F32),
            V((ntp, 2, rank, rows), F32),
            V((ndp, 2, rank, piece), F32),
            V((ndp, 2, rank, piece), F32),
            V((rows, shard), BF16),
            V((2, 2, rows, shard), BF16),
            V((2, 2, chunks, feats, CHUNK), BF16),
            V((2, 2, chunks, rows, CHUNK), F32),
            V((2, 2, chunks, rows, CHUNK), F32),
            dma((10, ndp)),
            dma((10, ndp)),
            dma((3, ntp)),
            dma((3, ntp)),
            dma((ntp,)),
            dma((width // piece,)),
            dma((3,)),
            dma((3,)),
            dma((chunks, ndp // 2)),
            dma((2, 2, chunks)),
            dma((2, 2, chunks)),
            dma((2, 2, chunks)),
        ],
        compiler_params=pltpu.CompilerParams(
            collective_id=0, has_side_effects=True, vmem_limit_bytes=60 * 2**20
        ),
    )(
        hidden,
        attention_norm_gain.reshape(1, model),
        query_key_value_weight[:, 0, :],
        key_value_cache[:, :, 0, :],
        cache_fill_lengths,
        output_weight_frozen[0],
        adapter_down_transposed[:, 0, :],
        adapter_up_matrix[:, 0, :],
        attention_rows,
        upstream,
        rewards,
        prompt_group_index,
        completion_live_lengths,
    )
    return dec, out, ga[:, None, :], gb[:, None, :]


def shards(
    hidden,
    attention_norm_gain,
    query_key_value_weight,
    key_value_cache,
    cache_fill_lengths,
    output_weight_frozen,
    adapter_down_transposed,
    adapter_up_matrix,
    attention_rows,
    upstream,
    rewards,
    prompt_group_index,
    completion_live_lengths,
):
    a_piece, b_piece = (
        lax.all_gather(adapter_down_transposed, "dp", axis=2, tiled=True),
        lax.all_gather(adapter_up_matrix, "dp", axis=2, tiled=True),
    )
    b_whole = lax.all_gather(b_piece, "tp", axis=1, tiled=True)
    up_matrix_flat = b_whole.reshape(b_whole.shape[0], -1).astype(jnp.float32)
    a_local = a_piece[:, 0, :]
    up_matrix_columns = b_piece[:, 0, :]
    w_rows = query_key_value_weight[:, 0, :].astype(jnp.float32)
    w_cols = output_weight_frozen[0]
    query_width = HEADS_TP * HD
    local_rolls = hidden.shape[0]
    decode_state = hidden.astype(jnp.float32)
    keys_new = []
    values_new = []
    for step in range(2):
        normed = rms_norm(decode_state, attention_norm_gain)
        spread = lax.all_to_all(normed, "dp", split_axis=1, concat_axis=0, tiled=True)
        partial_value = jnp.dot(spread, w_rows, precision=lax.Precision.HIGHEST)
        qkv = lax.psum_scatter(partial_value, "dp", scatter_dimension=0, tiled=True)
        query = qkv[:, :query_width].reshape(local_rolls, HEADS_TP, HD)
        keys_new.append(qkv[:, query_width : query_width + HD])
        values_new.append(qkv[:, query_width + HD :])
        attended = attend(
            query,
            key_value_cache[:, :, 0, :],
            cache_fill_lengths,
            jnp.stack(keys_new, axis=1),
            jnp.stack(values_new, axis=1),
        )
        columns = jnp.dot(
            lax.all_gather(attended, "dp", axis=0, tiled=True),
            w_cols,
            preferred_element_type=jnp.float32,
        )
        returned_values = lax.all_to_all(columns, "dp", split_axis=0, concat_axis=1, tiled=True)
        low_rank_decode = jnp.dot(attended, a_local.T, preferred_element_type=jnp.float32)
        state_update = returned_values + adapter_scale * jnp.dot(
            low_rank_decode, up_matrix_flat, precision=lax.Precision.HIGHEST
        )
        decode_state = decode_state + lax.psum(state_update, "tp")
    groups = local_rolls * lax.axis_size("dp") // GROUP
    onehot = (prompt_group_index[:, None] == jnp.arange(groups, dtype=jnp.int32)[None, :]).astype(
        jnp.float32
    )
    totals, squares = lax.psum(
        (
            jnp.sum(onehot * rewards[:, None], axis=0),
            jnp.sum(onehot * (rewards * rewards)[:, None], axis=0),
        ),
        "dp",
    )
    mean = totals / GROUP
    std = jnp.sqrt(jnp.maximum(squares / GROUP - mean * mean, 0.09))
    advantage = (rewards - jnp.sum(onehot * mean[None, :], axis=1)) / jnp.sum(
        onehot * std[None, :], axis=1
    )
    per_roll = advantage / completion_live_lengths.astype(jnp.float32)
    rows = attention_rows.shape[0]
    slot = jnp.arange(rows, dtype=jnp.int32) % COMP
    limit = jnp.repeat(completion_live_lengths, COMP)
    row_w = jnp.where(slot < limit, jnp.repeat(per_roll, COMP), 0.0)
    whole_rows = jnp.dot(
        attention_rows,
        lax.all_gather(output_weight_frozen, "dp", axis=2, tiled=True)[0],
        preferred_element_type=jnp.float32,
    )
    frozen_output_rows = lax.psum_scatter(whole_rows, "tp", scatter_dimension=1, tiled=True)
    low_sum = lax.psum(jnp.dot(attention_rows, a_local.T, preferred_element_type=jnp.float32), "tp")
    low_rank_rows = low_sum.astype(jnp.bfloat16)
    adapted_output_rows = frozen_output_rows + adapter_scale * jnp.dot(
        low_rank_rows, up_matrix_columns, preferred_element_type=jnp.float32
    )
    advantage_weighted = (row_w[:, None] * upstream.astype(jnp.float32)).astype(jnp.bfloat16)
    backward_result = lax.psum(
        jnp.dot(advantage_weighted, up_matrix_columns.T, preferred_element_type=jnp.float32), "tp"
    ).astype(jnp.bfloat16)
    down_gradient = adapter_scale * lax.dot_general(
        backward_result,
        attention_rows,
        (((0,), (0,)), ((), ())),
        preferred_element_type=jnp.float32,
    )
    up_gradient = adapter_scale * lax.dot_general(
        low_rank_rows,
        advantage_weighted,
        (((0,), (0,)), ((), ())),
        preferred_element_type=jnp.float32,
    )
    grad_a_part, grad_b_part = (
        lax.psum_scatter(down_gradient[:, None, :], "dp", scatter_dimension=2, tiled=True),
        lax.psum_scatter(up_gradient[:, None, :], "dp", scatter_dimension=2, tiled=True),
    )
    return (decode_state, adapted_output_rows, grad_a_part, grad_b_part)


def solution(mesh):
    placed = (
        P("dp", None),
        P(),
        P("dp", "tp", None),
        P("dp", None, "tp", None),
        P("dp"),
        P("tp", None, "dp"),
        P(None, "tp", "dp"),
        P(None, "tp", "dp"),
        P("dp", "tp"),
        P("dp", "tp"),
        P("dp"),
        P("dp"),
        P("dp"),
    )
    ndp, ntp = mesh.shape["dp"], mesh.shape["tp"]

    def body(*args):
        width = args[5].shape[2]
        piece = args[6].shape[2]
        if ntp == 4 and ndp == 8 and piece % 128 == 0 and width % CHUNK == 0:
            return fused_shards(ndp, ntp, *args)
        return shards(*args)

    return jax.shard_map(
        body,
        mesh=mesh,
        in_specs=placed,
        out_specs=(P("dp", None), P("dp", "tp"), P(None, "tp", "dp"), P(None, "tp", "dp")),
        check_vma=False,
    )
```

profile of v0, /device:TPU:29, one launch (start us, length us, event | category | flops | bytes accessed | tf_op | source)
XLA Modules:
  0.0 156.9 jit_solution(2144567989117692435)
XLA Ops:
  0.6 1.3 reshape.11.refs_1_
  1.9 149.1 %shard_map.156 = (f32[2,4096]{1,0:T(2,128)}, f32[512,1024]{1,0:T(8,128)}, f32[64,128]{1,0:T(8,128)}, f32[64,128]{1,0:T(8,128)}) custom-call(bf16[2,4096]{1,0:T(2,128)(2,1)} %refs_0_.1, bf16[1,4096]{1,0:T(2,128)(2,1)} %reshape.11.refs_1_, bf16[512,1280]{1,0:T(8,128)(2,1)} %bitcast.12, bf16[2,2048,256]{2,1,0:T(8,128)(2,1)} %bitcast.11, s32[2]{0:T(128)} %refs_4_.1, ...), custom_call_target="tpu_custom_call" | custom-call | tf_op jit(solution)/shard_map/pallas_call | solution.py:544
  151.1 1.4 copy.23
  152.5 0.0 copy-start.1
  152.5 0.0 copy-start
  152.5 3.2 %copy.24 = f32[512,1024]{1,0:T(8,128)} copy(f32[512,1024]{1,0:T(8,128)} %get-tuple-element.21) | data formatting | bytes 4194304
  155.6 0.0 copy-done.1
  155.6 0.6 copy.25
  156.3 0.0 copy-done
  156.3 0.6 copy.26
Async XLA Ops:
  152.5 3.2 %copy-start.1 = (f32[64,128]{1,0:T(8,128)S(1)}, f32[64,128]{1,0:T(8,128)}, u32[]{:S(2)}) copy-start(f32[64,128]{1,0:T(8,128)} %get-tuple-element.10) | copy-start | bytes 98308
  152.5 3.8 %copy-start = (f32[64,128]{1,0:T(8,128)S(1)}, f32[64,128]{1,0:T(8,128)}, u32[]{:S(2)}) copy-start(f32[64,128]{1,0:T(8,128)} %get-tuple-element.11) | copy-start | bytes 98308
where the time goes:
time: 157 us
  Pallas kernels  149 us (95%)
  local copies, waits for them, and re-layouts  7.09 us (5%)
    pallas_call x1, Pallas kernels, fused_shards(): pl.pallas_call(lambda *refs: fused_kernel(ndp, ntp, *refs), out_shape=(ja...  149 us
    unnamed x8, local copies, waits for them, and re-layouts  5.78 us

commit v1 on v0

--- a/solution.py
+++ b/solution.py
@@ -51,7 +51,7 @@
 NT = (((1,), (1,)), ((), ()))
 TN = (((0,), (0,)), ((), ()))
 CHUNK = 256
-LINE_PARTS = 8
+SEGS = 4
 ROW_PARTS = 8
 
 
@@ -114,8 +114,11 @@
     frecv,
     lbsend,
     lbrecv,
+    gown,
     gsend,
     grecv,
+    gzsend,
+    gzrecv,
     wt_ref,
     xbuf,
     wbuf,
@@ -133,6 +136,10 @@
     wl_r,
     ps_s,
     ps_r,
+    gy_s,
+    gy_r,
+    gz_s,
+    gz_r,
 ):
     d = lax.axis_index("dp")
     t = lax.axis_index("tp")
@@ -239,6 +246,8 @@
 
     def row_send(k):
         part = rows // ROW_PARTS
+        if k >= ROW_PARTS:
+            return
         seg = pl.ds(k * part, part)
         send(
             x_ref.at[seg], xbuf.at[y, c, seg], xs_s.at[1], xs_r.at[1], (other_y, t)
@@ -252,43 +261,176 @@
             xbuf.at[1 - y, c], xbuf.at[1 - y, dst_core], xs_s.at[2], xs_r.at[2], (d, mate)
         )
 
-    def line(ch, off, seg):
-        zt = (z + off) % nz
-        cols = pl.ds(ch * CHUNK, CHUNK)
+    feats = wo_ref.shape[0]
+    pieces = chunks * SEGS
+    near, far = z // 2, 1 - z // 2
+    end = jnp.logical_or(z == 0, z == nz - 1)
+    role_m = jnp.logical_and(jnp.logical_not(end), c == z // 2)
+    role_2 = jnp.logical_and(jnp.logical_not(end), c != z // 2)
+    z_up, z_dn = jnp.minimum(z + 1, nz - 1), jnp.maximum(z - 1, 0)
+    z_in = jnp.where(z < 2, z_up, z_dn)
+    z_out = jnp.where(z < 2, z_dn, z_up)
+
+    def seg_of(k):
+        size = feats // SEGS
+        return k // SEGS, pl.ds((k % SEGS) * size, size)
+
+    def own(k, which, zt):
+        ch, seg = seg_of(k)
         return send(
-            wo_ref.at[seg, cols],
+            wo_ref.at[seg, pl.ds(ch * CHUNK, CHUNK)],
             wbuf.at[z // 2, c, ch, seg],
-            wl_s.at[ch, off],
-            wl_r.at[z // 2, c, ch],
+            wl_s.at[which],
+            wl_r.at[z // 2, c, k],
             (2 * zt + y, 2 * x + z % 2),
         )
 
-    def quantum(k):
-        ch, part = k // LINE_PARTS, k % LINE_PARTS
-        size = wo_ref.shape[0] // LINE_PARTS
-        seg = pl.ds(part * size, size)
-        for off in (1, 3, 2):
-            line(ch, off, seg).start()
+    def hop(blk, j, which, zt):
+        k, cc = j // 2, j % 2
+        ch, seg = seg_of(k)
+        ref = wbuf.at[blk, cc, ch, seg]
+        return send(ref, ref, wl_s.at[which], wl_r.at[blk, cc, k], (2 * zt + y, t))
+
+    def own_tick(k):
+        @pl.when(z < nz - 1)
+        def _():
+            own(k, 0, z_up).start()
+
+        @pl.when(z > 0)
+        def _():
+            own(k, 1, z_dn).start()
 
         @pl.when(z % 2 != c)
         def _():
-            line(ch, 0, seg).start()
-
-    pending = list(range(chunks * LINE_PARTS))
-    row_parts = list(range(ROW_PARTS))
-
-    def bulk(n, m=0):
-        for _ in range(min(n, len(pending))):
-            quantum(pending.pop(0))
-        for _ in range(min(m, len(row_parts))):
-            row_send(row_parts.pop(0))
-
-    bulk(1, 1)
+            own(k, 2, z).start()
+
+    waited = {"near": 0, "far_m": 0, "far_2": 0}
+
+    def arrive(name, blk, upto):
+        for j in range(waited[name], upto):
+            hop(blk, j, 3, z_in).wait_recv()
+        waited[name] = max(waited[name], upto)
+
+    def relay_tick(name, blk, lo, hi, which, zt):
+        hi = min(hi, 2 * pieces)
+        arrive(name, blk, hi)
+        for j in range(lo, hi):
+            hop(blk, j, which, zt).start()
+
+    clock = [0]
+    ticks = pieces + 2 + 2 * pieces
+
+    def tick():
+        n = clock[0]
+        if n >= ticks:
+            return
+        clock[0] += 1
+        if n < pieces:
+            own_tick(n)
+            row_send(n)
+            return
+        m = n - pieces
+
+        @pl.when(role_m)
+        def _():
+            if m < pieces:
+                relay_tick("near", near, 2 * m, 2 * m + 2, 3, z_in)
+            if m < 2:
+                relay_tick("far_m", far, 2 * m, 2 * m + 2, 4, z_out)
+            elif m + 2 < 2 * pieces:
+                relay_tick("far_m", far, m + 2, m + 3, 4, z_out)
+
+        if m >= 2:
+
+            @pl.when(role_2)
+            def _():
+                relay_tick("far_2", far, m - 2, m - 1, 4, z_out)
+
+    def pump(n):
+        for _ in range(n):
+            tick()
+
+    pump(2)
 
     @pl.when(z % 2 == c)
     def _():
         for ch in range(chunks):
             wbuf[z // 2, c, ch] = wo_ref[:, ch * CHUNK : (ch + 1) * CHUNK]
+
+    def g_side():
+        return send(gsend.at[1 - y], grecv, gy_s, gy_r, (other_y, t))
+
+    def g_line(off):
+        zt = (z + off) % nz
+        return send(gzsend.at[zt], gzrecv.at[z], gz_s.at[off], gz_r.at[off], (2 * zt + y, t))
+
+    def share(dx, dy, ch):
+        zz = jnp.where(dx == 1, 1 - x, x)
+        yy = jnp.where(dy == 1, 1 - y, y)
+        return send(
+            pbuf.at[dx, dy, ch],
+            prcv.at[dx, dy, ch],
+            ps_s.at[dx, dy, ch],
+            ps_r.at[dx, dy, ch],
+            (2 * z + yy, 2 * zz + c),
+        )
+
+    def rows_in():
+        rows_whole().wait_recv()
+        relay(c).start()
+
+    def rows_ready():
+        send(x_ref, xbuf.at[y, 1 - c], xs_s.at[0], xs_r.at[0], (d, mate)).wait_recv()
+        relay(1 - c).wait_recv()
+
+    def unit(blk, ch):
+        is_near = blk is near
+        upto = 2 * (ch + 1) * SEGS
+        if is_near:
+
+            @pl.when(role_m)
+            def _():
+                arrive("near", blk, upto)
+
+            others = jnp.logical_not(role_m)
+        else:
+
+            @pl.when(role_m)
+            def _():
+                arrive("far_m", blk, upto)
+
+            @pl.when(role_2)
+            def _():
+                arrive("far_2", blk, upto)
+
+            others = end
+        for cc in range(2):
+            mine = jnp.logical_and(c + 2 * blk == z, c == cc)
+
+            @pl.when(jnp.logical_and(others, jnp.logical_not(mine)))
+            def _():
+                for k in range(ch * SEGS, (ch + 1) * SEGS):
+                    hop(blk, 2 * k + cc, 3, z_in).wait_recv()
+
+        dx = jnp.where(blk == x, 0, 1)
+        for dy in (1, 0):
+            yy = (y + dy) % 2
+            p = jnp.dot(xbuf[yy, 0], wbuf[blk, 0, ch], preferred_element_type=F32)
+            p = p + jnp.dot(xbuf[yy, 1], wbuf[blk, 1, ch], preferred_element_type=F32)
+            if dy == 1:
+                pbuf[dx, 1, ch] = p.astype(BF16)
+                share(dx, 1, ch).start()
+            else:
+
+                @pl.when(dx == 1)
+                def _():
+                    pbuf[1, 0, ch] = p.astype(BF16)
+                    share(1, 0, ch).start()
+
+                @pl.when(dx == 0)
+                def _():
+                    cols = pl.ds(pl.multiple_of((y * chunks + ch) * CHUNK, CHUNK), CHUNK)
+                    out_ref[:, cols] += p
 
     dp_wait(0, lambda p: hsend.at[p], hbuf)
     state = rows_of(hbuf, ndp)
@@ -303,7 +445,7 @@
         for i in range(ndp):
             qsend[step, i] = both[i * rolls : (i + 1) * rolls]
         dp_start(4 + 2 * step, lambda p: qsend.at[step, p], qrecv.at[step])
-        bulk(1, 2)
+        pump(2)
         qrecv[step, d] = qsend[step, d]
         if step == 0:
             dp_wait(1, lambda p: a_ref, abuf)
@@ -326,8 +468,8 @@
                 row_w = jnp.where(slot < live, adv / live, 0.0)
                 seg = pl.ds(r * COMP, COMP)
                 wt_ref[seg, :] = (row_w * up_ref[seg, :].astype(F32)).astype(BF16)
-            lbsend[0] = lax.dot_general(at, x_ref[...], NT, preferred_element_type=F32)
-            lbsend[1] = lax.dot_general(bt, wt_ref[...], NT, preferred_element_type=F32)
+            lbsend[0] = lax.dot_general(at, x_ref[...], NT, preferred_element_type=F32).astype(BF16)
+            lbsend[1] = lax.dot_general(bt, wt_ref[...], NT, preferred_element_type=F32).astype(BF16)
         dp_wait(4 + 2 * step, lambda p: qsend.at[step, p], qrecv.at[step])
         total = qrecv[step, 0]
         for i in range(1, ndp):
@@ -363,23 +505,29 @@
                 [att[h : h + 1] for h in range(HEADS_TP)], axis=1
             )
         dp_start(5 + 2 * step, lambda p: asend.at[step], arecv.at[step])
-        bulk(1, 1)
+        pump(2)
         arecv[step, d] = asend[step]
         if step == 0:
             tp_start(2, lbsend, lbrecv)
             lbrecv[t] = lbsend[...]
         else:
             tp_wait(2, lbsend, lbrecv)
-            lb = lbrecv[0]
+            lb = lbrecv[0].astype(F32)
             for i in range(1, ntp):
-                lb = lb + lbrecv[i]
+                lb = lb + lbrecv[i].astype(F32)
             lb = lb.astype(BF16)
             low_t, back_t = lb[0], lb[1]
             ga = adapter_scale * jnp.dot(back_t, x_ref[...], preferred_element_type=F32)
             gb = adapter_scale * jnp.dot(low_t, wt_ref[...], preferred_element_type=F32)
             for i in range(ndp):
-                gsend[i, 0] = ga[:, i * piece : (i + 1) * piece]
-                gsend[i, 1] = gb[:, i * piece : (i + 1) * piece]
+                for k, g in enumerate((ga, gb)):
+                    part = g[:, i * piece : (i + 1) * piece]
+                    gown[i % 2, i // 2, k] = part
+                    gsend[i % 2, i // 2, k] = part.astype(BF16)
+            g_side().start()
+            out_ref[...] = adapter_scale * lax.dot_general(
+                low_t, bt, TN, preferred_element_type=F32
+            )
         dp_wait(5 + 2 * step, lambda p: asend.at[step], arecv.at[step])
         attended = rows_of(arecv.at[step], ndp).astype(BF16)
         usend[step, :, :width] = jnp.dot(attended, wo_ref[...], preferred_element_type=F32)
@@ -391,7 +539,7 @@
             axis=1,
         )
         tp_start(step, usend.at[step], urecv.at[step])
-        bulk(1, 1)
+        pump(2)
         urecv[step, t] = usend[step]
         if step == 0:
             src_t = d // half
@@ -416,72 +564,31 @@
         fsend[i] = state[i * rolls : (i + 1) * rolls]
     dp_start(8, lambda p: fsend.at[p], frecv)
     frecv[d] = fsend[d]
-    dp_start(9, lambda p: gsend.at[p], grecv)
-    grecv[d] = gsend[d]
-    bulk(len(pending), len(row_parts))
-    rows_whole().wait_recv()
-    relay(c).start()
-    out_ref[...] = adapter_scale * lax.dot_general(low_t, bt, TN, preferred_element_type=F32)
-    send(x_ref, xbuf.at[y, 1 - c], xs_s.at[0], xs_r.at[0], (d, mate)).wait_recv()
+    rows_in()
+    g_side().wait_recv()
+    for i in range(nz):
+        gzsend[i] = (gown[y, i] + grecv[i].astype(F32)).astype(BF16)
+    for off in range(1, nz):
+        g_line(off).start()
+    pump(2)
+    rows_ready()
+    unit(near, 0)
+    pump(2)
+    unit(near, 1)
+    pump(2)
     dp_wait(8, lambda p: fsend.at[p], frecv)
     for i in range(ndp):
         dec_ref[:, i * width : (i + 1) * width] = frecv[i]
-    relay(1 - c).wait_recv()
-
-    def share(dx, dy, ch):
-        zz = jnp.where(dx == 1, 1 - x, x)
-        yy = jnp.where(dy == 1, 1 - y, y)
-        return send(
-            pbuf.at[dx, dy, ch],
-            prcv.at[dx, dy, ch],
-            ps_s.at[dx, dy, ch],
-            ps_r.at[dx, dy, ch],
-            (2 * z + yy, 2 * zz + c),
-        )
-
-    def stage(q, _):
-        ch, r = q // 4, q % 4
-        dx, dy = 1 - r // 2, 1 - r % 2
-        zz = jnp.where(dx == 1, 1 - x, x)
-        yy = jnp.where(dy == 1, 1 - y, y)
-
-        @pl.when(dy == 1)
-        def _():
-            for cc in range(2):
-                mine = jnp.logical_and(c + 2 * zz == z, c == cc)
-
-                @pl.when(jnp.logical_not(mine))
-                def _():
-                    send(
-                        wo_ref.at[:, pl.ds(0, CHUNK)],
-                        wbuf.at[zz, cc, ch],
-                        wl_s.at[0, 0],
-                        wl_r.at[zz, cc, ch],
-                        (d, mate),
-                    ).wait_recv()
-
-        p = jnp.dot(xbuf[yy, 0], wbuf[zz, 0, ch], preferred_element_type=F32)
-        p = p + jnp.dot(xbuf[yy, 1], wbuf[zz, 1, ch], preferred_element_type=F32)
-        last = r == 3
-
-        @pl.when(jnp.logical_not(last))
-        def _():
-            pbuf[dx, dy, ch] = p
-            share(dx, dy, ch).start()
-
-        @pl.when(last)
-        def _():
-            cols = pl.ds(pl.multiple_of((y * chunks + ch) * CHUNK, CHUNK), CHUNK)
-            out_ref[:, cols] += p
-
-        return 0
-
-    lax.fori_loop(0, 4 * chunks, stage, 0)
-
-    dp_wait(9, lambda p: gsend.at[p], grecv)
-    g = grecv[0]
-    for i in range(1, ndp):
-        g = g + grecv[i]
+    while waited["far_2"] < pieces or clock[0] < pieces + 2 + pieces:
+        pump(1)
+    unit(far, 0)
+    pump(ticks)
+    unit(far, 1)
+
+    g = gown[y, z] + grecv[z].astype(F32)
+    for off in range(1, nz):
+        g_line(off).wait_recv()
+        g = g + gzrecv[(z + nz - off) % nz].astype(F32)
     ga_ref[...] = g[0]
     gb_ref[...] = g[1]
     for ch in range(chunks):
@@ -489,21 +596,39 @@
             share(dx, dy, ch).wait_recv()
             yy = (y + dy) % 2
             cols = pl.ds(pl.multiple_of((yy * chunks + ch) * CHUNK, CHUNK), CHUNK)
-            out_ref[:, cols] += prcv[dx, dy, ch]
-
-    whole = pl.ds(0, wo_ref.shape[0])
+            out_ref[:, cols] += prcv[dx, dy, ch].astype(F32)
+
+    def drain(which, full):
+        send(full, full, wl_s.at[which], wl_r.at[0, 0, 0], (d, mate)).wait_send()
+
+    @pl.when(z < nz - 1)
+    def _():
+        drain(0, wbuf.at[0, 0])
+
+    @pl.when(z > 0)
+    def _():
+        drain(1, wbuf.at[0, 0])
+
+    @pl.when(z % 2 != c)
+    def _():
+        drain(2, wbuf.at[0, 0])
+
+    @pl.when(role_m)
+    def _():
+        drain(3, wbuf.at[0])
+
+    @pl.when(jnp.logical_not(end))
+    def _():
+        drain(4, wbuf.at[0])
+
     for ch in range(chunks):
-        for off in range(1, nz):
-            line(ch, off, whole).wait_send()
-
-        @pl.when(z % 2 != c)
-        def _():
-            line(ch, 0, whole).wait_send()
-
         for dx, dy in ((1, 0), (0, 1), (1, 1)):
             share(dx, dy, ch).wait_send()
     rows_whole().wait_send()
     relay(c).wait_send()
+    g_side().wait_send()
+    for off in range(1, nz):
+        g_line(off).wait_send()
 
     @pl.when(bdst != d)
     def _():
@@ -567,15 +692,18 @@
             V((2, ntp, ndp * rolls, width + 128), F32),
             V((ndp, rolls, width), F32),
             V((ndp, rolls, width), F32),
-            V((2, rank, rows), F32),
-            V((ntp, 2, rank, rows), F32),
-            V((ndp, 2, rank, piece), F32),
-            V((ndp, 2, rank, piece), F32),
+            V((2, rank, rows), BF16),
+            V((ntp, 2, rank, rows), BF16),
+            V((2, ndp // 2, 2, rank, piece), F32),
+            V((2, ndp // 2, 2, rank, piece), BF16),
+            V((ndp // 2, 2, rank, piece), BF16),
+            V((ndp // 2, 2, rank, piece), BF16),
+            V((ndp // 2, 2, rank, piece), BF16),
             V((rows, shard), BF16),
             V((2, 2, rows, shard), BF16),
             V((2, 2, chunks, feats, CHUNK), BF16),
-            V((2, 2, chunks, rows, CHUNK), F32),
-            V((2, 2, chunks, rows, CHUNK), F32),
+            V((2, 2, chunks, rows, CHUNK), BF16),
+            V((2, 2, chunks, rows, CHUNK), BF16),
             dma((10, ndp)),
             dma((10, ndp)),
             dma((3, ntp)),
@@ -584,10 +712,14 @@
             dma((width // piece,)),
             dma((3,)),
             dma((3,)),
-            dma((chunks, ndp // 2)),
+            dma((5,)),
+            dma((2, 2, chunks * SEGS)),
             dma((2, 2, chunks)),
             dma((2, 2, chunks)),
-            dma((2, 2, chunks)),
+            dma,
+            dma,
+            dma((ndp // 2,)),
+            dma((ndp // 2,)),
         ],
         compiler_params=pltpu.CompilerParams(
             collective_id=0, has_side_effects=True, vmem_limit_bytes=60 * 2**20

time: 157 us -> 114 us (0.73)
  the two profiles are of different devices: /device:TPU:29 before, /device:TPU:3 now
where the time goes in v1:
time: 114 us
  Pallas kernels  106 us (93%)
  local copies, waits for them, and re-layouts  7.09 us (6%)
    pallas_call x1, Pallas kernels, fused_shards(): pl.pallas_call(lambda *refs: fused_kernel(ndp, ntp, *refs), out_shape=(ja...  106 us
    unnamed x8, local copies, waits for them, and re-layouts  5.78 us

profile of v1, /device:TPU:3, one launch (start us, length us, event | category | flops | bytes accessed | tf_op | source)
XLA Modules:
  0.0 114.1 jit_solution(14565129777642018494)
XLA Ops:
  0.6 1.3 %reshape.11.refs_1_ = bf16[1,4096]{1,0:T(2,128)(2,1)} reshape(bf16[4096]{0:T(1024)(128)(2,1)} %param.14) | data formatting | bytes 16384 | tf_op jit(solution)/shard_map/reshape | solution.py:729
  1.9 106.4 %shard_map.156 = (f32[2,4096]{1,0:T(2,128)}, f32[512,1024]{1,0:T(8,128)}, f32[64,128]{1,0:T(8,128)}, f32[64,128]{1,0:T(8,128)}) custom-call(bf16[2,4096]{1,0:T(2,128)(2,1)} %refs_0_.1, bf16[1,4096]{1,0:T(2,128)(2,1)} %reshape.11.refs_1_, bf16[512,1280]{1,0:T(8,128)(2,1)} %bitcast.12, bf16[2,2048,256]{2,1,0:T(8,128)(2,1)} %bitcast.11, s32[2]{0:T(128)} %refs_4_.1, ...), custom_call_target="tpu_custom_call" | custom-call | tf_op jit(solution)/shard_map/pallas_call | solution.py:669
  108.4 1.4 %copy.23 = f32[2,4096]{1,0:T(2,128)} copy(f32[2,4096]{1,0:T(2,128)} %get-tuple-element.20) | data formatting | bytes 65536
  109.7 0.0 copy-start.1
  109.7 0.0 copy-start
  109.7 3.2 %copy.24 = f32[512,1024]{1,0:T(8,128)} copy(f32[512,1024]{1,0:T(8,128)} %get-tuple-element.21) | data formatting | bytes 4194304
  112.9 0.0 copy-done.1
  112.9 0.6 copy.25
  113.5 0.0 copy-done
  113.5 0.6 copy.26
Async XLA Ops:
  109.7 3.2 %copy-start.1 = (f32[64,128]{1,0:T(8,128)S(1)}, f32[64,128]{1,0:T(8,128)}, u32[]{:S(2)}) copy-start(f32[64,128]{1,0:T(8,128)} %get-tuple-element.10) | copy-start | bytes 98308
  109.7 3.8 %copy-start = (f32[64,128]{1,0:T(8,128)S(1)}, f32[64,128]{1,0:T(8,128)}, u32[]{:S(2)}) copy-start(f32[64,128]{1,0:T(8,128)} %get-tuple-element.11) | copy-start | bytes 98308

commit v2 on v1

--- a/solution.py
+++ b/solution.py
@@ -82,14 +82,14 @@
     ntp,
     h_ref,
     gain_ref,
-    wqkv_ref,
-    cache_ref,
+    wqkv_in,
+    cache_in,
     lens_ref,
-    wo_ref,
+    wo_in,
     a_ref,
     b_ref,
-    x_ref,
-    up_ref,
+    x_in,
+    up_in,
     rew_ref,
     idx_ref,
     live_ref,
@@ -101,7 +101,6 @@
     stats_ref,
     hbuf,
     abuf,
-    bbuf,
     bdbuf,
     statbuf,
     qsend,
@@ -113,7 +112,8 @@
     fsend,
     frecv,
     lbsend,
-    lbrecv,
+    lbhalf,
+    lbfull,
     gown,
     gsend,
     grecv,
@@ -140,6 +140,16 @@
     gy_r,
     gz_s,
     gz_r,
+    lb_s,
+    lb_r,
+    ab_s,
+    ab_r,
+    wo_ref,
+    x_ref,
+    wqkv_ref,
+    cache_ref,
+    up_ref,
+    in_s,
 ):
     d = lax.axis_index("dp")
     t = lax.axis_index("tp")
@@ -154,6 +164,18 @@
     qkvw = wqkv_ref.shape[1]
     rows = x_ref.shape[0]
 
+    def fetch(k):
+        src, dst = (
+            (wo_in, wo_ref),
+            (x_in, x_ref),
+            (wqkv_in, wqkv_ref),
+            (cache_in, cache_ref),
+            (up_in, up_ref),
+        )[k]
+        return pltpu.make_async_copy(src, dst, in_s.at[k])
+
+    for k in range(5):
+        fetch(k).start()
     barrier = pltpu.get_barrier_semaphore()
     for i in range(ndp):
         for j in range(ntp):
@@ -210,10 +232,14 @@
 
     dp_start(0, lambda p: hsend.at[p], hbuf)
     hbuf[d] = hsend[d]
-    dp_start(1, lambda p: a_ref, abuf)
-    abuf[d] = a_ref[...]
-    dp_start(2, lambda p: b_ref, bbuf)
-    bbuf[d] = b_ref[...]
+    abuf[y, z, 0] = a_ref[...]
+    abuf[y, z, 1] = b_ref[...]
+    for k, ref in enumerate((a_ref, b_ref)):
+        for off in range(1, nz):
+            peer = 2 * ((z + off) % nz) + y
+            cp = send(ref, abuf.at[y, z, k], ab_s.at[k, off], ab_r.at[k, off], (peer, t))
+            cp.start()
+            sent.append(cp)
     dp_start(3, lambda p: stats_ref, statbuf)
     statbuf[d] = stats_ref[...]
     per = width // piece
@@ -239,6 +265,8 @@
             sent.append(cp)
     mate = 2 * x + (1 - c)
     other_y = 2 * z + (1 - y)
+    fetch(0).wait()
+    fetch(1).wait()
     xcp = send(x_ref, xbuf.at[y, c], xs_s.at[0], xs_r.at[0], (d, mate))
     xcp.start()
     sent.append(xcp)
@@ -357,6 +385,18 @@
         for ch in range(chunks):
             wbuf[z // 2, c, ch] = wo_ref[:, ch * CHUNK : (ch + 1) * CHUNK]
 
+    def ab_side(yy):
+        return send(abuf.at[yy], abuf.at[yy], ab_s.at[0, 0], ab_r.at[0, 0], (other_y, t))
+
+    def lb_core():
+        return send(lbsend.at[1 - c], lbhalf.at[2], lb_s.at[0], lb_r.at[0], (d, mate))
+
+    def lb_chip():
+        return send(lbhalf.at[0], lbhalf.at[1], lb_s.at[1], lb_r.at[1], (d, 2 * (1 - x) + c))
+
+    def lb_back(core):
+        return send(lbfull.at[core], lbfull.at[core], lb_s.at[2], lb_r.at[2], (d, mate))
+
     def g_side():
         return send(gsend.at[1 - y], grecv, gy_s, gy_r, (other_y, t))
 
@@ -434,7 +474,16 @@
 
     dp_wait(0, lambda p: hsend.at[p], hbuf)
     state = rows_of(hbuf, ndp)
-    gain = gain_ref[:, pl.ds(pl.multiple_of(d * width, width), width)].astype(F32)
+    gains = gain_ref[...].astype(F32)
+    line = lax.broadcasted_iota(jnp.int32, gains.shape, 0)
+    gain = jnp.concatenate(
+        [
+            jnp.sum(jnp.where(line == d * (width // 128) + i, gains, 0.0), axis=0, keepdims=True)
+            for i in range(width // 128)
+        ],
+        axis=1,
+    )
+    fetch(2).wait()
     new_k, new_v = [], []
     factor = 1.0 / math.sqrt(HD)
 
@@ -447,17 +496,25 @@
         dp_start(4 + 2 * step, lambda p: qsend.at[step, p], qrecv.at[step])
         pump(2)
         qrecv[step, d] = qsend[step, d]
+        if step == 1:
+            lb_chip().wait_recv()
+            lbfull[c] = (lbhalf[0] + lbhalf[1]).astype(BF16)
+            lb_back(c).start()
         if step == 0:
-            dp_wait(1, lambda p: a_ref, abuf)
-            at = lanes_of(abuf, ndp)
-            dp_wait(2, lambda p: b_ref, bbuf)
-            bt = lanes_of(bbuf, ndp)
+            for k in range(2):
+                for off in range(1, nz):
+                    frm = (z + nz - off) % nz
+                    send(
+                        a_ref, abuf.at[y, frm, k], ab_s.at[k, off], ab_r.at[k, off], (2 * frm + y, t)
+                    ).wait_recv()
+            ab_side(y).start()
             dp_wait(3, lambda p: stats_ref, statbuf)
             tot = statbuf[0]
             for i in range(1, ndp):
                 tot = tot + statbuf[i]
             mean = tot[0:1] / GROUP
             std = jnp.sqrt(jnp.maximum(tot[1:2] / GROUP - mean * mean, 0.09))
+            fetch(4).wait()
             for r in range(rolls):
                 one, rew = ones[r], rew_ref[r]
                 live = live_ref[r].astype(F32)
@@ -468,8 +525,6 @@
                 row_w = jnp.where(slot < live, adv / live, 0.0)
                 seg = pl.ds(r * COMP, COMP)
                 wt_ref[seg, :] = (row_w * up_ref[seg, :].astype(F32)).astype(BF16)
-            lbsend[0] = lax.dot_general(at, x_ref[...], NT, preferred_element_type=F32).astype(BF16)
-            lbsend[1] = lax.dot_general(bt, wt_ref[...], NT, preferred_element_type=F32).astype(BF16)
         dp_wait(4 + 2 * step, lambda p: qsend.at[step, p], qrecv.at[step])
         total = qrecv[step, 0]
         for i in range(1, ndp):
@@ -477,6 +532,8 @@
         qkv = total[:, :qkvw] * lax.rsqrt(total[:, qkvw : qkvw + 1] / model + 1e-05)
         new_k.append(qkv[:, HEADS_TP * HD : HEADS_TP * HD + HD])
         new_v.append(qkv[:, HEADS_TP * HD + HD :])
+        if step == 0:
+            fetch(3).wait()
         for b in range(rolls):
             q = jnp.concatenate(
                 [qkv[b : b + 1, h * HD : (h + 1) * HD] for h in range(HEADS_TP)], axis=0
@@ -508,15 +565,20 @@
         pump(2)
         arecv[step, d] = asend[step]
         if step == 0:
-            tp_start(2, lbsend, lbrecv)
-            lbrecv[t] = lbsend[...]
+            ab_side(1 - y).wait_recv()
+            at, bt = (
+                jnp.concatenate([abuf[i % 2, i // 2, k] for i in range(ndp)], axis=1)
+                for k in range(2)
+            )
+            for k, (m, v) in enumerate(((at, x_ref), (bt, wt_ref))):
+                lb = lax.dot_general(m, v[...], NT, preferred_element_type=F32)
+                for i in range(2):
+                    lbsend[i, k] = lb[:, i * (rows // 2) : (i + 1) * (rows // 2)]
+            lb_core().start()
         else:
-            tp_wait(2, lbsend, lbrecv)
-            lb = lbrecv[0].astype(F32)
-            for i in range(1, ntp):
-                lb = lb + lbrecv[i].astype(F32)
-            lb = lb.astype(BF16)
-            low_t, back_t = lb[0], lb[1]
+            lb_back(c).wait_send()
+            lb_back(1 - c).wait_recv()
+            low_t, back_t = lanes_of(lbfull.at[:, 0], 2), lanes_of(lbfull.at[:, 1], 2)
             ga = adapter_scale * jnp.dot(back_t, x_ref[...], preferred_element_type=F32)
             gb = adapter_scale * jnp.dot(low_t, wt_ref[...], preferred_element_type=F32)
             for i in range(ndp):
@@ -542,6 +604,9 @@
         pump(2)
         urecv[step, t] = usend[step]
         if step == 0:
+            lb_core().wait_recv()
+            lbhalf[0] = lbsend[c] + lbhalf[2]
+            lb_chip().start()
             src_t = d // half
             for j in range(per):
                 frm = (d % half) * per + j
@@ -627,6 +692,9 @@
     rows_whole().wait_send()
     relay(c).wait_send()
     g_side().wait_send()
+    lb_core().wait_send()
+    lb_chip().wait_send()
+    ab_side(y).wait_send()
     for off in range(1, nz):
         g_line(off).wait_send()
 
@@ -656,6 +724,7 @@
     completion_live_lengths,
 ):
     rolls, model = hidden.shape
+    slots = key_value_cache.shape[1]
     width = model // ndp
     rank, _, piece = adapter_down_transposed.shape
     rows, shard = attention_rows.shape
@@ -664,24 +733,24 @@
     chunks = width // CHUNK
     vm = pl.BlockSpec(memory_space=pltpu.VMEM)
     sm = pl.BlockSpec(memory_space=pltpu.SMEM)
+    hbm = pl.BlockSpec(memory_space=pltpu.HBM)
     dma = pltpu.SemaphoreType.DMA
     V = pltpu.VMEM
     dec, out, ga, gb = pl.pallas_call(
         lambda *refs: fused_kernel(ndp, ntp, *refs),
         out_shape=(
-            jax.ShapeDtypeStruct((rolls, model), F32),
-            jax.ShapeDtypeStruct((rows, shard), F32),
-            jax.ShapeDtypeStruct((rank, piece), F32),
-            jax.ShapeDtypeStruct((rank, piece), F32),
+            pltpu.VMEM((rolls, model), F32),
+            pltpu.VMEM((rows, shard), F32),
+            pltpu.VMEM((rank, piece), F32),
+            pltpu.VMEM((rank, piece), F32),
         ),
-        in_specs=[vm, vm, vm, vm, sm, vm, vm, vm, vm, vm, sm, sm, sm],
+        in_specs=[vm, vm, hbm, hbm, sm, hbm, vm, vm, hbm, hbm, sm, sm, sm],
         out_specs=(vm, vm, vm, vm),
         scratch_shapes=[
             V((ndp, rolls, width), F32),
             V((8, 128), F32),
             V((ndp, rolls, width), F32),
-            V((ndp, rank, piece), BF16),
-            V((ndp, rank, piece), BF16),
+            V((2, ndp // 2, 2, rank, piece), BF16),
             V((width // piece, rank, piece), BF16),
             V((ndp, 8, 128), F32),
             V((2, ndp, rolls, qkvw + 128), F32),
@@ -692,8 +761,9 @@
             V((2, ntp, ndp * rolls, width + 128), F32),
             V((ndp, rolls, width), F32),
             V((ndp, rolls, width), F32),
-            V((2, rank, rows), BF16),
-            V((ntp, 2, rank, rows), BF16),
+            V((2, 2, rank, rows // 2), F32),
+            V((3, 2, rank, rows // 2), F32),
+            V((2, 2, rank, rows // 2), BF16),
             V((2, ndp // 2, 2, rank, piece), F32),
             V((2, ndp // 2, 2, rank, piece), BF16),
             V((ndp // 2, 2, rank, piece), BF16),
@@ -720,13 +790,23 @@
             dma,
             dma((ndp // 2,)),
             dma((ndp // 2,)),
+            dma((3,)),
+            dma((3,)),
+            dma((2, ndp // 2)),
+            dma((2, ndp // 2)),
+            V((feats, width), BF16),
+            V((rows, shard), BF16),
+            V((width, qkvw), BF16),
+            V((rolls, slots, 2 * HD), BF16),
+            V((rows, shard), BF16),
+            dma((5,)),
         ],
         compiler_params=pltpu.CompilerParams(
-            collective_id=0, has_side_effects=True, vmem_limit_bytes=60 * 2**20
+            collective_id=0, has_side_effects=True, vmem_limit_bytes=64815104
         ),
     )(
         hidden,
-        attention_norm_gain.reshape(1, model),
+        attention_norm_gain.reshape(model // 128, 128),
         query_key_value_weight[:, 0, :],
         key_value_cache[:, :, 0, :],
         cache_fill_lengths,

time: 114 us -> 104 us (0.912)
  Pallas kernels: 106 us -> 100 us
  local copies, waits for them, and re-layouts: 7.09 us -> 3.16 us
    pallas_call x1, Pallas kernels: 106 us -> 100 us  [fused_shards(): pl.pallas_call(lambda *refs: fused_kernel(ndp, ntp, *refs), out_shape=(pl...]
    unnamed x8 -> x4, local copies, waits for them, and re-layouts: 5.78 us -> 3.16 us
    reshape x1 -> x0, local copies, waits for them, and re-layouts: 1.31 us -> none  [fused_shards(): attention_norm_gain.reshape(1, model)]
where the time goes in v2:
time: 104 us
  Pallas kernels  100 us (96%)
  local copies, waits for them, and re-layouts  3.16 us (3%)
    pallas_call x1, Pallas kernels, fused_shards(): pl.pallas_call(lambda *refs: fused_kernel(ndp, ntp, *refs), out_shape=(pl...  100 us
    unnamed x4, local copies, waits for them, and re-layouts  3.16 us

profile of v2, /device:TPU:3, one launch (start us, length us, event | category | flops | bytes accessed | tf_op | source)
XLA Modules:
  0.0 104.0 jit_solution(5605351967495783579)
XLA Ops:
  0.6 100.2 %shard_map.156 = (f32[2,4096]{1,0:T(2,128)S(1)}, f32[512,1024]{1,0:T(8,128)S(1)}, f32[64,128]{1,0:T(8,128)S(1)}, f32[64,128]{1,0:T(8,128)S(1)}) custom-call(bf16[2,4096]{1,0:T(2,128)(2,1)} %refs_0_.1, bf16[32,128]{1,0:T(8,128)(2,1)} %bitcast.19, bf16[512,1280]{1,0:T(8,128)(2,1)} %bitcast.15, bf16[2,2048,256]{2,1,0:T(8,128)(2,1)} %bitcast.14, s32[2]{0:T(128)} %refs_4_.1, ...), custom_call_target="tpu_custom_call" | custom-call | tf_op jit(solution)/shard_map/pallas_call | solution.py:739
  100.9 0.6 copy.23
  101.5 0.6 copy.25
  102.1 0.6 copy.26
  102.7 1.3 %copy.24 = f32[512,1024]{1,0:T(8,128)} copy(f32[512,1024]{1,0:T(8,128)S(1)} %get-tuple-element.17) | data formatting | bytes 4194304

commit v3 on v2

--- a/solution.py
+++ b/solution.py
@@ -93,10 +93,10 @@
     rew_ref,
     idx_ref,
     live_ref,
-    dec_ref,
-    out_ref,
-    ga_ref,
-    gb_ref,
+    dec_out,
+    rows_out,
+    ga_out,
+    gb_out,
     hsend,
     stats_ref,
     hbuf,
@@ -150,6 +150,12 @@
     cache_ref,
     up_ref,
     in_s,
+    out_ref,
+    dec_ref,
+    ga_ref,
+    gb_ref,
+    out_s,
+    fin_s,
 ):
     d = lax.axis_index("dp")
     t = lax.axis_index("tp")
@@ -163,6 +169,8 @@
     chunks = wo_ref.shape[1] // CHUNK
     qkvw = wqkv_ref.shape[1]
     rows = x_ref.shape[0]
+    mate = 2 * x + (1 - c)
+    other_y = 2 * z + (1 - y)
 
     def fetch(k):
         src, dst = (
@@ -199,26 +207,24 @@
     def dp_start(e, src, dst):
         for off in range(1, ndp):
             peer = (d + off) % ndp
-            cp = send(src(peer), dst.at[d], ds_s.at[e, off], ds_r.at[e, off], (peer, t))
-            cp.start()
-            sent.append(cp)
-
-    def dp_wait(e, src, dst):
-        for off in range(1, ndp):
-            frm = (d + ndp - off) % ndp
-            send(src(d), dst.at[frm], ds_s.at[e, off], ds_r.at[e, off], (frm, t)).wait_recv()
+            send(src(peer), dst.at[d], ds_s.at[e], ds_r.at[e], (peer, t)).start()
+        whole = dst.at[pl.ds(0, ndp - 1)]
+        sent.append(send(whole, whole, ds_s.at[e], ds_r.at[e], (d, (t + 1) % ntp)))
+
+    def dp_wait(e, dst):
+        whole = dst.at[pl.ds(0, ndp - 1)]
+        send(whole, whole, ds_s.at[e], ds_r.at[e], (d, (t + 1) % ntp)).wait_recv()
 
     def tp_start(e, src, dst):
         for off in range(1, ntp):
             peer = (t + off) % ntp
-            cp = send(src, dst.at[t], ts_s.at[e, off], ts_r.at[e, off], (d, peer))
-            cp.start()
-            sent.append(cp)
-
-    def tp_wait(e, src, dst):
-        for off in range(1, ntp):
-            frm = (t + ntp - off) % ntp
-            send(src, dst.at[frm], ts_s.at[e, off], ts_r.at[e, off], (d, frm)).wait_recv()
+            send(src, dst.at[t], ts_s.at[e], ts_r.at[e], (d, peer)).start()
+        whole = dst.at[pl.ds(0, ntp - 1)]
+        sent.append(send(whole, whole, ts_s.at[e], ts_r.at[e], (d, (t + 1) % ntp)))
+
+    def tp_wait(e, dst):
+        whole = dst.at[pl.ds(0, ntp - 1)]
+        send(whole, whole, ts_s.at[e], ts_r.at[e], (d, (t + 1) % ntp)).wait_recv()
 
     hidden = h_ref[...].astype(F32)
     for i in range(ndp):
@@ -237,10 +243,10 @@
     for k, ref in enumerate((a_ref, b_ref)):
         for off in range(1, nz):
             peer = 2 * ((z + off) % nz) + y
-            cp = send(ref, abuf.at[y, z, k], ab_s.at[k, off], ab_r.at[k, off], (peer, t))
-            cp.start()
-            sent.append(cp)
-    dp_start(3, lambda p: stats_ref, statbuf)
+            send(ref, abuf.at[y, z, k], ab_s.at[0], ab_r.at[0], (peer, t)).start()
+    others = abuf.at[0, pl.ds(0, nz - 1)]
+    sent.append(send(others, others, ab_s.at[0], ab_r.at[0], (other_y, t)))
+    dp_start(1, lambda p: stats_ref, statbuf)
     statbuf[d] = stats_ref[...]
     per = width // piece
     half = ndp // per
@@ -260,11 +266,9 @@
                 send(b_ref, bdbuf.at[bslot], bd_s.at[0], bd_r.at[bslot], (bdst, tj)).start()
 
         else:
-            cp = send(b_ref, bdbuf.at[bslot], bd_s.at[j], bd_r.at[bslot], (bdst, tj))
-            cp.start()
-            sent.append(cp)
-    mate = 2 * x + (1 - c)
-    other_y = 2 * z + (1 - y)
+            send(b_ref, bdbuf.at[bslot], bd_s.at[1], bd_r.at[bslot], (bdst, tj)).start()
+    copies = bdbuf.at[pl.ds(0, ntp - 1)]
+    sent.append(send(copies, copies, bd_s.at[1], bd_r.at[0], (other_y, t)))
     fetch(0).wait()
     fetch(1).wait()
     xcp = send(x_ref, xbuf.at[y, c], xs_s.at[0], xs_r.at[0], (d, mate))
@@ -299,15 +303,24 @@
     z_in = jnp.where(z < 2, z_up, z_dn)
     z_out = jnp.where(z < 2, z_dn, z_up)
 
+    cuts = [(ch, 0, CHUNK) for ch in range(chunks - 1)]
+    cuts += [(chunks - 1, h * 128, 128) for h in range(CHUNK // 128)]
+
     def seg_of(k):
-        size = feats // SEGS
-        return k // SEGS, pl.ds((k % SEGS) * size, size)
+        ch, part = k // SEGS, k % SEGS
+        if ch < chunks - 1:
+            size = feats // SEGS
+            return ch, pl.ds(part * size, size), 0, CHUNK
+        halves = CHUNK // 128
+        size = feats * halves // SEGS
+        per_half = SEGS // halves
+        return ch, pl.ds((part % per_half) * size, size), (part // per_half) * 128, 128
 
     def own(k, which, zt):
-        ch, seg = seg_of(k)
+        ch, seg, off, num = seg_of(k)
         return send(
-            wo_ref.at[seg, pl.ds(ch * CHUNK, CHUNK)],
-            wbuf.at[z // 2, c, ch, seg],
+            wo_ref.at[seg, pl.ds(ch * CHUNK + off, num)],
+            wbuf.at[z // 2, c, ch, seg, pl.ds(off, num)],
             wl_s.at[which],
             wl_r.at[z // 2, c, k],
             (2 * zt + y, 2 * x + z % 2),
@@ -315,8 +328,8 @@
 
     def hop(blk, j, which, zt):
         k, cc = j // 2, j % 2
-        ch, seg = seg_of(k)
-        ref = wbuf.at[blk, cc, ch, seg]
+        ch, seg, off, num = seg_of(k)
+        ref = wbuf.at[blk, cc, ch, seg, pl.ds(off, num)]
         return send(ref, ref, wl_s.at[which], wl_r.at[blk, cc, k], (2 * zt + y, t))
 
     def own_tick(k):
@@ -346,7 +359,7 @@
             hop(blk, j, which, zt).start()
 
     clock = [0]
-    ticks = pieces + 2 + 2 * pieces
+    ticks = 3 * pieces
 
     def tick():
         n = clock[0]
@@ -363,16 +376,13 @@
         def _():
             if m < pieces:
                 relay_tick("near", near, 2 * m, 2 * m + 2, 3, z_in)
-            if m < 2:
                 relay_tick("far_m", far, 2 * m, 2 * m + 2, 4, z_out)
-            elif m + 2 < 2 * pieces:
-                relay_tick("far_m", far, m + 2, m + 3, 4, z_out)
-
-        if m >= 2:
+
+        if m >= pieces:
 
             @pl.when(role_2)
             def _():
-                relay_tick("far_2", far, m - 2, m - 1, 4, z_out)
+                relay_tick("far_2", far, 2 * (m - pieces), 2 * (m - pieces) + 2, 4, z_out)
 
     def pump(n):
         for _ in range(n):
@@ -386,7 +396,7 @@
             wbuf[z // 2, c, ch] = wo_ref[:, ch * CHUNK : (ch + 1) * CHUNK]
 
     def ab_side(yy):
-        return send(abuf.at[yy], abuf.at[yy], ab_s.at[0, 0], ab_r.at[0, 0], (other_y, t))
+        return send(abuf.at[yy], abuf.at[yy], ab_s.at[1], ab_r.at[1], (other_y, t))
 
     def lb_core():
         return send(lbsend.at[1 - c], lbhalf.at[2], lb_s.at[0], lb_r.at[0], (d, mate))
@@ -402,16 +412,22 @@
 
     def g_line(off):
         zt = (z + off) % nz
-        return send(gzsend.at[zt], gzrecv.at[z], gz_s.at[off], gz_r.at[off], (2 * zt + y, t))
-
-    def share(dx, dy, ch):
+        return send(gzsend.at[zt], gzrecv.at[z], gz_s, gz_r, (2 * zt + y, t))
+
+    def g_lines():
+        whole = gzrecv.at[pl.ds(0, nz - 1)]
+        return send(whole, whole, gz_s, gz_r, (other_y, t))
+
+    def share(dx, dy, u):
         zz = jnp.where(dx == 1, 1 - x, x)
         yy = jnp.where(dy == 1, 1 - y, y)
+        ch, off, num = cuts[u]
+        cols = pl.ds(off, num)
         return send(
-            pbuf.at[dx, dy, ch],
-            prcv.at[dx, dy, ch],
-            ps_s.at[dx, dy, ch],
-            ps_r.at[dx, dy, ch],
+            pbuf.at[2 * dx + dy, ch, :, cols],
+            prcv.at[2 * dx + dy, ch, :, cols],
+            ps_s,
+            ps_r.at[u],
             (2 * z + yy, 2 * zz + c),
         )
 
@@ -423,9 +439,24 @@
         send(x_ref, xbuf.at[y, 1 - c], xs_s.at[0], xs_r.at[0], (d, mate)).wait_recv()
         relay(1 - c).wait_recv()
 
-    def unit(blk, ch):
+    def columns(yy, u):
+        ch, off, num = cuts[u]
+        return pl.ds(pl.multiple_of((yy * chunks + ch) * CHUNK + off, 128), num)
+
+    def final(k):
+        src, dst = ((dec_ref, dec_out), (ga_ref, ga_out), (gb_ref, gb_out))[k]
+        return pltpu.make_async_copy(src, dst, fin_s.at[k])
+
+    def emit(dy, u):
+        cols = columns((y + dy) % 2, u)
+        return pltpu.make_async_copy(out_ref.at[:, cols], rows_out.at[:, cols], out_s)
+
+    def unit(blk, u):
         is_near = blk is near
-        upto = 2 * (ch + 1) * SEGS
+        ch, off, num = cuts[u]
+        cols = pl.ds(off, num)
+        own_ks = [k for k in range(pieces) if seg_of(k)[0] == ch and seg_of(k)[2] == off]
+        upto = 2 * (max(own_ks) + 1)
         if is_near:
 
             @pl.when(role_m)
@@ -449,30 +480,29 @@
 
             @pl.when(jnp.logical_and(others, jnp.logical_not(mine)))
             def _():
-                for k in range(ch * SEGS, (ch + 1) * SEGS):
+                for k in own_ks:
                     hop(blk, 2 * k + cc, 3, z_in).wait_recv()
 
         dx = jnp.where(blk == x, 0, 1)
         for dy in (1, 0):
             yy = (y + dy) % 2
-            p = jnp.dot(xbuf[yy, 0], wbuf[blk, 0, ch], preferred_element_type=F32)
-            p = p + jnp.dot(xbuf[yy, 1], wbuf[blk, 1, ch], preferred_element_type=F32)
+            p = jnp.dot(xbuf[yy, 0], wbuf[blk, 0, ch, :, cols], preferred_element_type=F32)
+            p = p + jnp.dot(xbuf[yy, 1], wbuf[blk, 1, ch, :, cols], preferred_element_type=F32)
             if dy == 1:
-                pbuf[dx, 1, ch] = p.astype(BF16)
-                share(dx, 1, ch).start()
+                pbuf[2 * dx + 1, ch, :, cols] = p.astype(BF16)
+                share(dx, 1, u).start()
             else:
 
                 @pl.when(dx == 1)
                 def _():
-                    pbuf[1, 0, ch] = p.astype(BF16)
-                    share(1, 0, ch).start()
+                    pbuf[2, ch, :, cols] = p.astype(BF16)
+                    share(1, 0, u).start()
 
                 @pl.when(dx == 0)
                 def _():
-                    cols = pl.ds(pl.multiple_of((y * chunks + ch) * CHUNK, CHUNK), CHUNK)
-                    out_ref[:, cols] += p
-
-    dp_wait(0, lambda p: hsend.at[p], hbuf)
+                    out_ref[:, columns(y, u)] += p
+
+    dp_wait(0, hbuf)
     state = rows_of(hbuf, ndp)
     gains = gain_ref[...].astype(F32)
     line = lax.broadcasted_iota(jnp.int32, gains.shape, 0)
@@ -493,7 +523,7 @@
         both = jnp.concatenate([part, jnp.broadcast_to(squares, (ndp * rolls, 128))], axis=1)
         for i in range(ndp):
             qsend[step, i] = both[i * rolls : (i + 1) * rolls]
-        dp_start(4 + 2 * step, lambda p: qsend.at[step, p], qrecv.at[step])
+        dp_start(2 + 2 * step, lambda p: qsend.at[step, p], qrecv.at[step])
         pump(2)
         qrecv[step, d] = qsend[step, d]
         if step == 1:
@@ -501,14 +531,9 @@
             lbfull[c] = (lbhalf[0] + lbhalf[1]).astype(BF16)
             lb_back(c).start()
         if step == 0:
-            for k in range(2):
-                for off in range(1, nz):
-                    frm = (z + nz - off) % nz
-                    send(
-                        a_ref, abuf.at[y, frm, k], ab_s.at[k, off], ab_r.at[k, off], (2 * frm + y, t)
-                    ).wait_recv()
+            send(others, others, ab_s.at[0], ab_r.at[0], (other_y, t)).wait_recv()
             ab_side(y).start()
-            dp_wait(3, lambda p: stats_ref, statbuf)
+            dp_wait(1, statbuf)
             tot = statbuf[0]
             for i in range(1, ndp):
                 tot = tot + statbuf[i]
@@ -525,7 +550,7 @@
                 row_w = jnp.where(slot < live, adv / live, 0.0)
                 seg = pl.ds(r * COMP, COMP)
                 wt_ref[seg, :] = (row_w * up_ref[seg, :].astype(F32)).astype(BF16)
-        dp_wait(4 + 2 * step, lambda p: qsend.at[step, p], qrecv.at[step])
+        dp_wait(2 + 2 * step, qrecv.at[step])
         total = qrecv[step, 0]
         for i in range(1, ndp):
             total = total + qrecv[step, i]
@@ -561,7 +586,7 @@
             asend[step, b : b + 1, :] = jnp.concatenate(
                 [att[h : h + 1] for h in range(HEADS_TP)], axis=1
             )
-        dp_start(5 + 2 * step, lambda p: asend.at[step], arecv.at[step])
+        dp_start(3 + 2 * step, lambda p: asend.at[step], arecv.at[step])
         pump(2)
         arecv[step, d] = asend[step]
         if step == 0:
@@ -590,7 +615,7 @@
             out_ref[...] = adapter_scale * lax.dot_general(
                 low_t, bt, TN, preferred_element_type=F32
             )
-        dp_wait(5 + 2 * step, lambda p: asend.at[step], arecv.at[step])
+        dp_wait(3 + 2 * step, arecv.at[step])
         attended = rows_of(arecv.at[step], ndp).astype(BF16)
         usend[step, :, :width] = jnp.dot(attended, wo_ref[...], preferred_element_type=F32)
         usend[step, :, width:] = jnp.concatenate(
@@ -617,7 +642,7 @@
                     send(b_ref, bdbuf.at[j], bd_s.at[0], bd_r.at[j], (frm, src_t)).wait_recv()
 
             bd = lanes_of(bdbuf, per)
-        tp_wait(step, usend.at[step], urecv.at[step])
+        tp_wait(step, urecv.at[step])
         upd = urecv[step, 0]
         for i in range(1, ntp):
             upd = upd + urecv[step, i]
@@ -627,7 +652,7 @@
 
     for i in range(ndp):
         fsend[i] = state[i * rolls : (i + 1) * rolls]
-    dp_start(8, lambda p: fsend.at[p], frecv)
+    dp_start(6, lambda p: fsend.at[p], frecv)
     frecv[d] = fsend[d]
     rows_in()
     g_side().wait_recv()
@@ -637,31 +662,42 @@
         g_line(off).start()
     pump(2)
     rows_ready()
-    unit(near, 0)
-    pump(2)
-    unit(near, 1)
-    pump(2)
-    dp_wait(8, lambda p: fsend.at[p], frecv)
+    for u in range(len(cuts)):
+        unit(near, u)
+        pump(2)
+    dp_wait(6, frecv)
     for i in range(ndp):
         dec_ref[:, i * width : (i + 1) * width] = frecv[i]
-    while waited["far_2"] < pieces or clock[0] < pieces + 2 + pieces:
+    final(0).start()
+    for cp in sent:
+        cp.wait_send()
+    while clock[0] < 2 * pieces + pieces // 2:
         pump(1)
     unit(far, 0)
     pump(ticks)
-    unit(far, 1)
-
     g = gown[y, z] + grecv[z].astype(F32)
+    g_lines().wait_recv()
     for off in range(1, nz):
-        g_line(off).wait_recv()
         g = g + gzrecv[(z + nz - off) % nz].astype(F32)
     ga_ref[...] = g[0]
     gb_ref[...] = g[1]
-    for ch in range(chunks):
+    final(1).start()
+    final(2).start()
+    for u in range(1, len(cuts)):
+        unit(far, u)
+    for u in range(len(cuts)):
+        ch, off, num = cuts[u]
+        three = prcv.at[pl.ds(1, 3), ch, :, pl.ds(off, num)]
+        send(three, three, ps_s, ps_r.at[u], (d, mate)).wait_recv()
         for dx, dy in ((1, 0), (0, 1), (1, 1)):
-            share(dx, dy, ch).wait_recv()
-            yy = (y + dy) % 2
-            cols = pl.ds(pl.multiple_of((yy * chunks + ch) * CHUNK, CHUNK), CHUNK)
-            out_ref[:, cols] += prcv[dx, dy, ch].astype(F32)
+            got = prcv[2 * dx + dy, ch, :, pl.ds(off, num)].astype(F32)
+            out_ref[:, columns((y + dy) % 2, u)] += got
+        for dy in range(2):
+            emit(dy, u).start()
+
+    pltpu.make_async_copy(out_ref, rows_out, out_s).wait()
+    for k in range(3):
+        final(k).wait()
 
     def drain(which, full):
         send(full, full, wl_s.at[which], wl_r.at[0, 0, 0], (d, mate)).wait_send()
@@ -686,24 +722,19 @@
     def _():
         drain(4, wbuf.at[0])
 
-    for ch in range(chunks):
-        for dx, dy in ((1, 0), (0, 1), (1, 1)):
-            share(dx, dy, ch).wait_send()
+    three = pbuf.at[pl.ds(1, 3)]
+    send(three, three, ps_s, ps_r.at[0], (d, mate)).wait_send()
     rows_whole().wait_send()
     relay(c).wait_send()
     g_side().wait_send()
     lb_core().wait_send()
     lb_chip().wait_send()
     ab_side(y).wait_send()
-    for off in range(1, nz):
-        g_line(off).wait_send()
+    g_lines().wait_send()
 
     @pl.when(bdst != d)
     def _():
         send(b_ref, bdbuf.at[bslot], bd_s.at[0], bd_r.at[bslot], (bdst, t)).wait_send()
-
-    for cp in sent:
-        cp.wait_send()
 
 
 def fused_shards(
@@ -745,7 +776,7 @@
             pltpu.VMEM((rank, piece), F32),
         ),
         in_specs=[vm, vm, hbm, hbm, sm, hbm, vm, vm, hbm, hbm, sm, sm, sm],
-        out_specs=(vm, vm, vm, vm),
+        out_specs=(pl.BlockSpec(memory_space=pl.ANY),) * 4,
         scratch_shapes=[
             V((ndp, rolls, width), F32),
             V((8, 128), F32),
@@ -772,34 +803,40 @@
             V((rows, shard), BF16),
             V((2, 2, rows, shard), BF16),
             V((2, 2, chunks, feats, CHUNK), BF16),
-            V((2, 2, chunks, rows, CHUNK), BF16),
-            V((2, 2, chunks, rows, CHUNK), BF16),
-            dma((10, ndp)),
-            dma((10, ndp)),
-            dma((3, ntp)),
-            dma((3, ntp)),
-            dma((ntp,)),
+            V((4, chunks, rows, CHUNK), BF16),
+            V((4, chunks, rows, CHUNK), BF16),
+            dma((7,)),
+            dma((7,)),
+            dma((2,)),
+            dma((2,)),
+            dma((2,)),
             dma((width // piece,)),
             dma((3,)),
             dma((3,)),
             dma((5,)),
             dma((2, 2, chunks * SEGS)),
-            dma((2, 2, chunks)),
-            dma((2, 2, chunks)),
+            dma,
+            dma((chunks - 1 + CHUNK // 128,)),
             dma,
             dma,
-            dma((ndp // 2,)),
-            dma((ndp // 2,)),
+            dma,
+            dma,
             dma((3,)),
             dma((3,)),
-            dma((2, ndp // 2)),
-            dma((2, ndp // 2)),
+            dma((2,)),
+            dma((2,)),
             V((feats, width), BF16),
             V((rows, shard), BF16),
             V((width, qkvw), BF16),
             V((rolls, slots, 2 * HD), BF16),
             V((rows, shard), BF16),
             dma((5,)),
+            V((rows, shard), F32),
+            V((rolls, model), F32),
+            V((rank, piece), F32),
+            V((rank, piece), F32),
+            dma,
+            dma((3,)),
         ],
         compiler_params=pltpu.CompilerParams(
             collective_id=0, has_side_effects=True, vmem_limit_bytes=64815104

time: 104 us -> 98.9 us (0.951)
  Pallas kernels: 100 us -> 94.7 us
    pallas_call x1, Pallas kernels: 100 us -> 94.7 us  [fused_shards(): pl.pallas_call(lambda *refs: fused_kernel(ndp, ntp, *refs), out_shape=(pl...]
where the time goes in v3:
time: 98.9 us; the launch traced here: 98.5 us
  Pallas kernels  94.7 us (96%)
  local copies, waits for them, and re-layouts  3.16 us (3%)
    pallas_call x1, Pallas kernels, fused_shards(): pl.pallas_call(lambda *refs: fused_kernel(ndp, ntp, *refs), out_shape=(pl...  94.7 us
    unnamed x4, local copies, waits for them, and re-layouts  3.16 us

profile of v3, /device:TPU:3, one launch (start us, length us, event | category | flops | bytes accessed | tf_op | source)
XLA Modules:
  0.0 98.5 jit_solution(930018018045604314)
XLA Ops:
  0.6 94.7 %shard_map.156 = (f32[2,4096]{1,0:T(2,128)S(1)}, f32[512,1024]{1,0:T(8,128)S(1)}, f32[64,128]{1,0:T(8,128)S(1)}, f32[64,128]{1,0:T(8,128)S(1)}) custom-call(bf16[2,4096]{1,0:T(2,128)(2,1)} %refs_0_.1, bf16[32,128]{1,0:T(8,128)(2,1)} %bitcast.19, bf16[512,1280]{1,0:T(8,128)(2,1)} %bitcast.15, bf16[2,2048,256]{2,1,0:T(8,128)(2,1)} %bitcast.14, s32[2]{0:T(128)} %refs_4_.1, ...), custom_call_target="tpu_custom_call" | custom-call | tf_op jit(solution)/shard_map/pallas_call | solution.py:770
  95.4 0.6 copy.23
  96.0 0.6 copy.25
  96.6 0.6 copy.26
  97.2 1.3 %copy.24 = f32[512,1024]{1,0:T(8,128)} copy(f32[512,1024]{1,0:T(8,128)S(1)} %get-tuple-element.17) | data formatting | bytes 4194304

commit v4 on v3

--- a/solution.py
+++ b/solution.py
@@ -104,6 +104,8 @@
     bdbuf,
     statbuf,
     qsend,
+    qside,
+    qline,
     qrecv,
     asend,
     arecv,
@@ -156,6 +158,14 @@
     gb_ref,
     out_s,
     fin_s,
+    qy_s,
+    qy_r,
+    qz_s,
+    qz_r,
+    ay_s,
+    ay_r,
+    az_s,
+    az_r,
 ):
     d = lax.axis_index("dp")
     t = lax.axis_index("tp")
@@ -226,9 +236,8 @@
         whole = dst.at[pl.ds(0, ntp - 1)]
         send(whole, whole, ts_s.at[e], ts_r.at[e], (d, (t + 1) % ntp)).wait_recv()
 
-    hidden = h_ref[...].astype(F32)
     for i in range(ndp):
-        hsend[i] = hidden[:, i * width : (i + 1) * width]
+        hsend[i] = h_ref[:, i * width : (i + 1) * width]
     lane = lax.broadcasted_iota(jnp.int32, (1, 128), 1)
     ones = [jnp.where(lane == idx_ref[r], 1.0, 0.0) for r in range(rolls)]
     stats_ref[...] = jnp.zeros_like(stats_ref)
@@ -250,25 +259,11 @@
     statbuf[d] = stats_ref[...]
     per = width // piece
     half = ndp // per
-    bdst = t * half + d // per
-    bslot = d % per
-    for j in range(ntp):
-        tj = (t + j) % ntp
-        if j == 0:
-            here = bdst == d
-
-            @pl.when(here)
-            def _():
-                bdbuf[bslot] = b_ref[...]
-
-            @pl.when(jnp.logical_not(here))
-            def _():
-                send(b_ref, bdbuf.at[bslot], bd_s.at[0], bd_r.at[bslot], (bdst, tj)).start()
-
-        else:
-            send(b_ref, bdbuf.at[bslot], bd_s.at[1], bd_r.at[bslot], (bdst, tj)).start()
-    copies = bdbuf.at[pl.ds(0, ntp - 1)]
-    sent.append(send(copies, copies, bd_s.at[1], bd_r.at[0], (other_y, t)))
+    src_t = d // half
+
+    def up_block(tj):
+        return send(bdbuf, bdbuf, bd_s, bd_r, (d, tj))
+
     fetch(0).wait()
     fetch(1).wait()
     xcp = send(x_ref, xbuf.at[y, c], xs_s.at[0], xs_r.at[0], (d, mate))
@@ -394,6 +389,21 @@
     def _():
         for ch in range(chunks):
             wbuf[z // 2, c, ch] = wo_ref[:, ch * CHUNK : (ch + 1) * CHUNK]
+
+    def q_side(step):
+        return send(qsend.at[step, 1 - y], qside.at[step], qy_s.at[step], qy_r.at[step], (other_y, t))
+
+    def q_lines(step):
+        whole = qrecv.at[step, pl.ds(0, nz - 1)]
+        return send(whole, whole, qz_s.at[step], qz_r.at[step], (other_y, t))
+
+    def a_side(step, yy):
+        ref = arecv.at[step, yy]
+        return send(ref, ref, ay_s.at[step], ay_r.at[step], (other_y, t))
+
+    def a_lines(step):
+        whole = arecv.at[step, 0, pl.ds(0, nz - 1)]
+        return send(whole, whole, az_s.at[step], az_r.at[step], (other_y, t))
 
     def ab_side(yy):
         return send(abuf.at[yy], abuf.at[yy], ab_s.at[1], ab_r.at[1], (other_y, t))
@@ -503,7 +513,7 @@
                     out_ref[:, columns(y, u)] += p
 
     dp_wait(0, hbuf)
-    state = rows_of(hbuf, ndp)
+    state = jnp.concatenate([hbuf[i].astype(F32) for i in range(ndp)], axis=0)
     gains = gain_ref[...].astype(F32)
     line = lax.broadcasted_iota(jnp.int32, gains.shape, 0)
     gain = jnp.concatenate(
@@ -522,10 +532,9 @@
         part = exact_dot(state * gain, wqkv_ref[...])
         both = jnp.concatenate([part, jnp.broadcast_to(squares, (ndp * rolls, 128))], axis=1)
         for i in range(ndp):
-            qsend[step, i] = both[i * rolls : (i + 1) * rolls]
-        dp_start(2 + 2 * step, lambda p: qsend.at[step, p], qrecv.at[step])
-        pump(2)
-        qrecv[step, d] = qsend[step, d]
+            qsend[step, i % 2, i // 2] = both[i * rolls : (i + 1) * rolls]
+        q_side(step).start()
+        pump(1)
         if step == 1:
             lb_chip().wait_recv()
             lbfull[c] = (lbhalf[0] + lbhalf[1]).astype(BF16)
@@ -550,15 +559,24 @@
                 row_w = jnp.where(slot < live, adv / live, 0.0)
                 seg = pl.ds(r * COMP, COMP)
                 wt_ref[seg, :] = (row_w * up_ref[seg, :].astype(F32)).astype(BF16)
-        dp_wait(2 + 2 * step, qrecv.at[step])
-        total = qrecv[step, 0]
-        for i in range(1, ndp):
-            total = total + qrecv[step, i]
+        q_side(step).wait_recv()
+        for i in range(nz):
+            qline[step, i] = qsend[step, y, i] + qside[step, i]
+        for off in range(1, nz):
+            zt = (z + off) % nz
+            src, dst = qline.at[step, zt], qrecv.at[step, z]
+            send(src, dst, qz_s.at[step], qz_r.at[step], (2 * zt + y, t)).start()
+        pump(2)
+        q_lines(step).wait_recv()
+        total = qline[step, z]
+        for off in range(1, nz):
+            total = total + qrecv[step, (z + off) % nz]
         qkv = total[:, :qkvw] * lax.rsqrt(total[:, qkvw : qkvw + 1] / model + 1e-05)
         new_k.append(qkv[:, HEADS_TP * HD : HEADS_TP * HD + HD])
         new_v.append(qkv[:, HEADS_TP * HD + HD :])
         if step == 0:
             fetch(3).wait()
+        heads = []
         for b in range(rolls):
             q = jnp.concatenate(
                 [qkv[b : b + 1, h * HD : (h + 1) * HD] for h in range(HEADS_TP)], axis=0
@@ -582,19 +600,29 @@
             )
             for e, v in zip(ee, new_v):
                 att = att + (e / den).astype(BF16).astype(F32) * v[b : b + 1]
-            att = att.astype(BF16).astype(F32)
-            asend[step, b : b + 1, :] = jnp.concatenate(
-                [att[h : h + 1] for h in range(HEADS_TP)], axis=1
-            )
-        dp_start(3 + 2 * step, lambda p: asend.at[step], arecv.at[step])
-        pump(2)
-        arecv[step, d] = asend[step]
+            heads.append(jnp.concatenate([att[h : h + 1] for h in range(HEADS_TP)], axis=1))
+        asend[step] = jnp.concatenate(heads, axis=0).astype(BF16)
+        for off in range(1, nz):
+            zt = (z + off) % nz
+            send(
+                asend.at[step], arecv.at[step, y, z], az_s.at[step], az_r.at[step], (2 * zt + y, t)
+            ).start()
+        pump(1)
+        arecv[step, y, z] = asend[step]
         if step == 0:
             ab_side(1 - y).wait_recv()
             at, bt = (
                 jnp.concatenate([abuf[i % 2, i // 2, k] for i in range(ndp)], axis=1)
                 for k in range(2)
             )
+
+            @pl.when(t == src_t)
+            def _():
+                for j in range(per):
+                    bdbuf[j] = abuf[j % 2, (d % half) * (per // 2) + j // 2, 1]
+                for off in range(1, ntp):
+                    up_block((t + off) % ntp).start()
+
             for k, (m, v) in enumerate(((at, x_ref), (bt, wt_ref))):
                 lb = lax.dot_general(m, v[...], NT, preferred_element_type=F32)
                 for i in range(2):
@@ -615,8 +643,13 @@
             out_ref[...] = adapter_scale * lax.dot_general(
                 low_t, bt, TN, preferred_element_type=F32
             )
-        dp_wait(3 + 2 * step, arecv.at[step])
-        attended = rows_of(arecv.at[step], ndp).astype(BF16)
+        a_lines(step).wait_recv()
+        a_side(step, y).start()
+        pump(1)
+        a_side(step, 1 - y).wait_recv()
+        attended = jnp.concatenate(
+            [arecv[step, i % 2, i // 2].astype(F32) for i in range(ndp)], axis=0
+        ).astype(BF16)
         usend[step, :, :width] = jnp.dot(attended, wo_ref[...], preferred_element_type=F32)
         usend[step, :, width:] = jnp.concatenate(
             [
@@ -632,14 +665,10 @@
             lb_core().wait_recv()
             lbhalf[0] = lbsend[c] + lbhalf[2]
             lb_chip().start()
-            src_t = d // half
-            for j in range(per):
-                frm = (d % half) * per + j
-                same = jnp.logical_and(src_t == t, frm == d)
-
-                @pl.when(jnp.logical_not(same))
-                def _():
-                    send(b_ref, bdbuf.at[j], bd_s.at[0], bd_r.at[j], (frm, src_t)).wait_recv()
+
+            @pl.when(t != src_t)
+            def _():
+                up_block(src_t).wait_recv()
 
             bd = lanes_of(bdbuf, per)
         tp_wait(step, urecv.at[step])
@@ -652,7 +681,7 @@
 
     for i in range(ndp):
         fsend[i] = state[i * rolls : (i + 1) * rolls]
-    dp_start(6, lambda p: fsend.at[p], frecv)
+    dp_start(2, lambda p: fsend.at[p], frecv)
     frecv[d] = fsend[d]
     rows_in()
     g_side().wait_recv()
@@ -665,7 +694,7 @@
     for u in range(len(cuts)):
         unit(near, u)
         pump(2)
-    dp_wait(6, frecv)
+    dp_wait(2, frecv)
     for i in range(ndp):
         dec_ref[:, i * width : (i + 1) * width] = frecv[i]
     final(0).start()
@@ -727,14 +756,20 @@
     rows_whole().wait_send()
     relay(c).wait_send()
     g_side().wait_send()
+    for step in range(2):
+        q_side(step).wait_send()
+        q_lines(step).wait_send()
+        a_side(step, y).wait_send()
+        a_lines(step).wait_send()
     lb_core().wait_send()
     lb_chip().wait_send()
     ab_side(y).wait_send()
     g_lines().wait_send()
 
-    @pl.when(bdst != d)
+    @pl.when(t == src_t)
     def _():
-        send(b_ref, bdbuf.at[bslot], bd_s.at[0], bd_r.at[bslot], (bdst, t)).wait_send()
+        copies = wo_ref.at[pl.ds(0, (ntp - 1) * rank)]
+        send(copies, copies, bd_s, bd_r, (d, mate)).wait_send()
 
 
 def fused_shards(
@@ -778,16 +813,18 @@
         in_specs=[vm, vm, hbm, hbm, sm, hbm, vm, vm, hbm, hbm, sm, sm, sm],
         out_specs=(pl.BlockSpec(memory_space=pl.ANY),) * 4,
         scratch_shapes=[
-            V((ndp, rolls, width), F32),
-            V((8, 128), F32),
-            V((ndp, rolls, width), F32),
+            V((ndp, rolls, width), BF16),
+            V((2, 128), F32),
+            V((ndp, rolls, width), BF16),
             V((2, ndp // 2, 2, rank, piece), BF16),
             V((width // piece, rank, piece), BF16),
-            V((ndp, 8, 128), F32),
-            V((2, ndp, rolls, qkvw + 128), F32),
-            V((2, ndp, rolls, qkvw + 128), F32),
-            V((2, rolls, feats), F32),
-            V((2, ndp, rolls, feats), F32),
+            V((ndp, 2, 128), F32),
+            V((2, 2, ndp // 2, rolls, qkvw + 128), F32),
+            V((2, ndp // 2, rolls, qkvw + 128), F32),
+            V((2, ndp // 2, rolls, qkvw + 128), F32),
+            V((2, ndp // 2, rolls, qkvw + 128), F32),
+            V((2, rolls, feats), BF16),
+            V((2, 2, ndp // 2, rolls, feats), BF16),
             V((2, ndp * rolls, width + 128), F32),
             V((2, ntp, ndp * rolls, width + 128), F32),
             V((ndp, rolls, width), F32),
@@ -805,12 +842,12 @@
             V((2, 2, chunks, feats, CHUNK), BF16),
             V((4, chunks, rows, CHUNK), BF16),
             V((4, chunks, rows, CHUNK), BF16),
-            dma((7,)),
-            dma((7,)),
+            dma((3,)),
+            dma((3,)),
             dma((2,)),
             dma((2,)),
-            dma((2,)),
-            dma((width // piece,)),
+            dma,
+            dma,
             dma((3,)),
             dma((3,)),
             dma((5,)),
@@ -837,7 +874,8 @@
             V((rank, piece), F32),
             dma,
             dma((3,)),
-        ],
+        ]
+        + [dma((2,))] * 8,
         compiler_params=pltpu.CompilerParams(
             collective_id=0, has_side_effects=True, vmem_limit_bytes=64815104
         ),

time: 98.9 us -> 94.7 us (0.958)
  Pallas kernels: 94.7 us -> 90.7 us
    pallas_call x1, Pallas kernels: 94.7 us -> 90.7 us  [fused_shards(): pl.pallas_call(lambda *refs: fused_kernel(ndp, ntp, *refs), out_shape=(pl...]
where the time goes in v4:
time: 94.7 us; the launch traced here: 94.5 us
  Pallas kernels  90.7 us (96%)
  local copies, waits for them, and re-layouts  3.16 us (3%)
    pallas_call x1, Pallas kernels, fused_shards(): pl.pallas_call(lambda *refs: fused_kernel(ndp, ntp, *refs), out_shape=(pl...  90.7 us
    unnamed x4, local copies, waits for them, and re-layouts  3.16 us

profile of v4, /device:TPU:3, one launch (start us, length us, event | category | flops | bytes accessed | tf_op | source)
XLA Modules:
  0.0 94.5 jit_solution(8628059174945884630)
XLA Ops:
  0.6 90.7 %shard_map.156 = (f32[2,4096]{1,0:T(2,128)S(1)}, f32[512,1024]{1,0:T(8,128)S(1)}, f32[64,128]{1,0:T(8,128)S(1)}, f32[64,128]{1,0:T(8,128)S(1)}) custom-call(bf16[2,4096]{1,0:T(2,128)(2,1)} %refs_0_.1, bf16[32,128]{1,0:T(8,128)(2,1)} %bitcast.19, bf16[512,1280]{1,0:T(8,128)(2,1)} %bitcast.15, bf16[2,2048,256]{2,1,0:T(8,128)(2,1)} %bitcast.14, s32[2]{0:T(128)} %refs_4_.1, ...), custom_call_target="tpu_custom_call" | custom-call | tf_op jit(solution)/shard_map/pallas_call | solution.py:805
  91.4 0.6 copy.23
  92.0 0.6 copy.25
  92.6 0.6 copy.26
  93.2 1.3 %copy.24 = f32[512,1024]{1,0:T(8,128)} copy(f32[512,1024]{1,0:T(8,128)S(1)} %get-tuple-element.17) | data formatting | bytes 4194304

commit v5 on v4

--- a/solution.py
+++ b/solution.py
@@ -158,6 +158,7 @@
     gb_ref,
     out_s,
     fin_s,
+    acc,
     qy_s,
     qy_r,
     qz_s,
@@ -294,6 +295,8 @@
     end = jnp.logical_or(z == 0, z == nz - 1)
     role_m = jnp.logical_and(jnp.logical_not(end), c == z // 2)
     role_2 = jnp.logical_and(jnp.logical_not(end), c != z // 2)
+    lead = jnp.where(c == near, far, near)
+    trail = 1 - lead
     z_up, z_dn = jnp.minimum(z + 1, nz - 1), jnp.maximum(z - 1, 0)
     z_in = jnp.where(z < 2, z_up, z_dn)
     z_out = jnp.where(z < 2, z_dn, z_up)
@@ -462,42 +465,40 @@
         return pltpu.make_async_copy(out_ref.at[:, cols], rows_out.at[:, cols], out_s)
 
     def unit(blk, u):
-        is_near = blk is near
         ch, off, num = cuts[u]
         cols = pl.ds(off, num)
         own_ks = [k for k in range(pieces) if seg_of(k)[0] == ch and seg_of(k)[2] == off]
         upto = 2 * (max(own_ks) + 1)
-        if is_near:
-
-            @pl.when(role_m)
-            def _():
-                arrive("near", blk, upto)
-
-            others = jnp.logical_not(role_m)
-        else:
-
-            @pl.when(role_m)
-            def _():
-                arrive("far_m", blk, upto)
+        leads = blk is lead
+
+        @pl.when(role_m)
+        def _():
+            arrive("far_m" if leads else "near", blk, upto)
+
+        if not leads:
 
             @pl.when(role_2)
             def _():
                 arrive("far_2", blk, upto)
 
-            others = end
-        for cc in range(2):
-            mine = jnp.logical_and(c + 2 * blk == z, c == cc)
-
-            @pl.when(jnp.logical_and(others, jnp.logical_not(mine)))
-            def _():
-                for k in own_ks:
-                    hop(blk, 2 * k + cc, 3, z_in).wait_recv()
+        others = jnp.logical_not(role_m) if leads else end
+        parts = [(k, cc) for k in own_ks for cc in range(2)]
+
+        def landed(todo):
+            for cc in range(2):
+                mine = jnp.logical_and(c + 2 * blk == z, c == cc)
+                ks = [k for k, core in todo if core == cc]
+
+                if ks:
+
+                    @pl.when(jnp.logical_and(others, jnp.logical_not(mine)))
+                    def _():
+                        for k in ks:
+                            hop(blk, 2 * k + cc, 3, z_in).wait_recv()
 
         dx = jnp.where(blk == x, 0, 1)
-        for dy in (1, 0):
-            yy = (y + dy) % 2
-            p = jnp.dot(xbuf[yy, 0], wbuf[blk, 0, ch, :, cols], preferred_element_type=F32)
-            p = p + jnp.dot(xbuf[yy, 1], wbuf[blk, 1, ch, :, cols], preferred_element_type=F32)
+
+        def put(dy, p):
             if dy == 1:
                 pbuf[2 * dx + 1, ch, :, cols] = p.astype(BF16)
                 share(dx, 1, u).start()
@@ -511,6 +512,29 @@
                 @pl.when(dx == 0)
                 def _():
                     out_ref[:, columns(y, u)] += p
+
+        if leads or u < len(cuts) - 1:
+            landed(parts)
+            for dy in (1, 0):
+                yy = (y + dy) % 2
+                p = jnp.dot(xbuf[yy, 0], wbuf[blk, 0, ch, :, cols], preferred_element_type=F32)
+                p = p + jnp.dot(xbuf[yy, 1], wbuf[blk, 1, ch, :, cols], preferred_element_type=F32)
+                put(dy, p)
+            return
+        for i, (k, cc) in enumerate(parts):
+            landed([(k, cc)])
+            seg = seg_of(k)[1]
+            for dy in (1, 0):
+                yy = (y + dy) % 2
+                p = jnp.dot(
+                    xbuf[yy, cc, :, seg], wbuf[blk, cc, ch, seg, cols], preferred_element_type=F32
+                )
+                if i:
+                    p = p + acc[dy]
+                if i < len(parts) - 1:
+                    acc[dy] = p
+                else:
+                    put(dy, p)
 
     dp_wait(0, hbuf)
     state = jnp.concatenate([hbuf[i].astype(F32) for i in range(ndp)], axis=0)
@@ -687,12 +711,10 @@
     g_side().wait_recv()
     for i in range(nz):
         gzsend[i] = (gown[y, i] + grecv[i].astype(F32)).astype(BF16)
-    for off in range(1, nz):
-        g_line(off).start()
     pump(2)
     rows_ready()
     for u in range(len(cuts)):
-        unit(near, u)
+        unit(lead, u)
         pump(2)
     dp_wait(2, frecv)
     for i in range(ndp):
@@ -702,18 +724,13 @@
         cp.wait_send()
     while clock[0] < 2 * pieces + pieces // 2:
         pump(1)
-    unit(far, 0)
+    unit(trail, 0)
     pump(ticks)
-    g = gown[y, z] + grecv[z].astype(F32)
-    g_lines().wait_recv()
+    unit(trail, 1)
     for off in range(1, nz):
-        g = g + gzrecv[(z + nz - off) % nz].astype(F32)
-    ga_ref[...] = g[0]
-    gb_ref[...] = g[1]
-    final(1).start()
-    final(2).start()
-    for u in range(1, len(cuts)):
-        unit(far, u)
+        g_line(off).start()
+    for u in range(2, len(cuts)):
+        unit(trail, u)
     for u in range(len(cuts)):
         ch, off, num = cuts[u]
         three = prcv.at[pl.ds(1, 3), ch, :, pl.ds(off, num)]
@@ -724,6 +741,14 @@
         for dy in range(2):
             emit(dy, u).start()
 
+    g = gown[y, z] + grecv[z].astype(F32)
+    g_lines().wait_recv()
+    for off in range(1, nz):
+        g = g + gzrecv[(z + nz - off) % nz].astype(F32)
+    ga_ref[...] = g[0]
+    gb_ref[...] = g[1]
+    final(1).start()
+    final(2).start()
     pltpu.make_async_copy(out_ref, rows_out, out_s).wait()
     for k in range(3):
         final(k).wait()
@@ -874,6 +899,7 @@
             V((rank, piece), F32),
             dma,
             dma((3,)),
+            V((2, rows, 128), F32),
         ]
         + [dma((2,))] * 8,
         compiler_params=pltpu.CompilerParams(

time: 94.7 us -> 92.1 us (0.973)
  Pallas kernels: 90.7 us -> 88.1 us
    pallas_call x1, Pallas kernels: 90.7 us -> 88.1 us  [fused_shards(): pl.pallas_call(lambda *refs: fused_kernel(ndp, ntp, *refs), out_shape=(pl...]
where the time goes in v5:
time: 92.1 us; the launch traced here: 91.9 us
  Pallas kernels  88.1 us (96%)
  local copies, waits for them, and re-layouts  3.16 us (3%)
    pallas_call x1, Pallas kernels, fused_shards(): pl.pallas_call(lambda *refs: fused_kernel(ndp, ntp, *refs), out_shape=(pl...  88.1 us
    unnamed x4, local copies, waits for them, and re-layouts  3.16 us

profile of v5, /device:TPU:3, one launch (start us, length us, event | category | flops | bytes accessed | tf_op | source)
XLA Modules:
  0.0 91.9 jit_solution(9366182123703364713)
XLA Ops:
  0.6 88.1 %shard_map.156 = (f32[2,4096]{1,0:T(2,128)S(1)}, f32[512,1024]{1,0:T(8,128)S(1)}, f32[64,128]{1,0:T(8,128)S(1)}, f32[64,128]{1,0:T(8,128)S(1)}) custom-call(bf16[2,4096]{1,0:T(2,128)(2,1)} %refs_0_.1, bf16[32,128]{1,0:T(8,128)(2,1)} %bitcast.19, bf16[512,1280]{1,0:T(8,128)(2,1)} %bitcast.15, bf16[2,2048,256]{2,1,0:T(8,128)(2,1)} %bitcast.14, s32[2]{0:T(128)} %refs_4_.1, ...), custom_call_target="tpu_custom_call" | custom-call | tf_op jit(solution)/shard_map/pallas_call | solution.py:830
  88.8 0.6 copy.23
  89.4 0.6 copy.25
  90.0 0.6 copy.26
  90.6 1.3 %copy.24 = f32[512,1024]{1,0:T(8,128)} copy(f32[512,1024]{1,0:T(8,128)S(1)} %get-tuple-element.17) | data formatting | bytes 4194304

commit v6 on v5

--- a/solution.py
+++ b/solution.py
@@ -795,6 +795,15 @@
     def _():
         copies = wo_ref.at[pl.ds(0, (ntp - 1) * rank)]
         send(copies, copies, bd_s, bd_r, (d, mate)).wait_send()
+
+
+def finish_kernel(*refs):
+    n = len(refs) // 2
+    copies = [pltpu.make_async_copy(refs[i], refs[n + i], refs[-1].at[i]) for i in range(n)]
+    for cp in copies:
+        cp.start()
+    for cp in copies:
+        cp.wait()
 
 
 def fused_shards(
@@ -920,7 +929,16 @@
         prompt_group_index,
         completion_live_lengths,
     )
-    return dec, out, ga[:, None, :], gb[:, None, :]
+    parts = (dec, out, ga[:, None, :], gb[:, None, :])
+    anywhere = (pl.BlockSpec(memory_space=pl.ANY),) * len(parts)
+    return pl.pallas_call(
+        finish_kernel,
+        out_shape=tuple(jax.ShapeDtypeStruct(p.shape, F32) for p in parts),
+        in_specs=[vm] * len(parts),
+        out_specs=anywhere,
+        scratch_shapes=[dma((len(parts),))],
+        compiler_params=pltpu.CompilerParams(vmem_limit_bytes=2**20),
+    )(*[pltpu.with_memory_space_constraint(p, pltpu.VMEM) for p in parts])
 
 
 def shards(

time: 92.1 us -> 90.3 us (0.980)
  local copies, waits for them, and re-layouts: 3.16 us -> 0 us
  Pallas kernels: 88.1 us -> 89.5 us
    unnamed x4 -> x0, local copies, waits for them, and re-layouts: 3.16 us -> none
    pallas_call x0 -> x1, Pallas kernels: none -> 1.37 us  [fused_shards(): pl.pallas_call(finish_kernel, out_shape=tuple((jax.ShapeDtypeStruct(p.sha...]
where the time goes in v6:
time: 90.3 us; the launch traced here: 90.1 us
  Pallas kernels  89.5 us (99%)
    pallas_call x1, Pallas kernels, fused_shards(): pl.pallas_call(lambda *refs: fused_kernel(ndp, ntp, *refs), out_shape=(pl...  88.1 us

profile of v6, /device:TPU:3, one launch (start us, length us, event | category | flops | bytes accessed | tf_op | source)
XLA Modules:
  0.0 90.1 jit_solution(16545559980390105761)
XLA Ops:
  0.6 88.1 %shard_map.156 = (f32[2,4096]{1,0:T(2,128)S(1)}, f32[512,1024]{1,0:T(8,128)S(1)}, f32[64,128]{1,0:T(8,128)S(1)}, f32[64,128]{1,0:T(8,128)S(1)}) custom-call(bf16[2,4096]{1,0:T(2,128)(2,1)} %refs_0_.1, bf16[32,128]{1,0:T(8,128)(2,1)} %bitcast.15, bf16[512,1280]{1,0:T(8,128)(2,1)} %bitcast.11, bf16[2,2048,256]{2,1,0:T(8,128)(2,1)} %bitcast.10, s32[2]{0:T(128)} %refs_4_.1, ...), custom_call_target="tpu_custom_call" | custom-call | tf_op jit(solution)/shard_map/pallas_call | solution.py:839
  88.8 1.4 %shard_map.157 = (f32[2,4096]{1,0:T(2,128)}, f32[512,1024]{1,0:T(8,128)}, f32[64,1,128]{2,1,0:T(1,128)}, f32[64,1,128]{2,1,0:T(1,128)}) custom-call(f32[2,4096]{1,0:T(2,128)S(1)} %get-tuple-element.8.refs_0_, f32[512,1024]{1,0:T(8,128)S(1)} %get-tuple-element.9.refs_1_, f32[64,1,128]{2,1,0:T(1,128)S(1)} %bitcast.8, f32[64,1,128]{2,1,0:T(1,128)S(1)} %bitcast.9), custom_call_target="tpu_custom_call" | custom-call | tf_op jit(solution)/shard_map/pallas_call | solution.py:934

commit v7 on v6

--- a/solution.py
+++ b/solution.py
@@ -80,19 +80,19 @@
 def fused_kernel(
     ndp,
     ntp,
-    h_ref,
-    gain_ref,
+    h_in,
+    gain_in,
     wqkv_in,
     cache_in,
-    lens_ref,
+    lens_in,
     wo_in,
-    a_ref,
-    b_ref,
+    a_in,
+    b_in,
     x_in,
     up_in,
-    rew_ref,
-    idx_ref,
-    live_ref,
+    rew_in,
+    idx_in,
+    live_in,
     dec_out,
     rows_out,
     ga_out,
@@ -119,8 +119,10 @@
     gown,
     gsend,
     grecv,
-    gzsend,
-    gzrecv,
+    gus,
+    gur,
+    gds,
+    gdr,
     wt_ref,
     xbuf,
     wbuf,
@@ -140,8 +142,10 @@
     ps_r,
     gy_s,
     gy_r,
-    gz_s,
-    gz_r,
+    gu_s,
+    gu_r,
+    gd_s,
+    gd_r,
     lb_s,
     lb_r,
     ab_s,
@@ -167,6 +171,14 @@
     ay_r,
     az_s,
     az_r,
+    h_ref,
+    gain_ref,
+    a_ref,
+    b_ref,
+    lens_ref,
+    rew_ref,
+    idx_ref,
+    live_ref,
 ):
     d = lax.axis_index("dp")
     t = lax.axis_index("tp")
@@ -190,11 +202,17 @@
             (wqkv_in, wqkv_ref),
             (cache_in, cache_ref),
             (up_in, up_ref),
+            (h_in, h_ref),
+            (a_in, a_ref),
+            (b_in, b_ref),
+            (idx_in, idx_ref),
+            (rew_in, rew_ref),
+            (gain_in, gain_ref),
+            (live_in, live_ref),
+            (lens_in, lens_ref),
         )[k]
         return pltpu.make_async_copy(src, dst, in_s.at[k])
 
-    for k in range(5):
-        fetch(k).start()
     barrier = pltpu.get_barrier_semaphore()
     for i in range(ndp):
         for j in range(ntp):
@@ -205,7 +223,11 @@
                     device_id=((d + i) % ndp, (t + j) % ntp),
                     device_id_type=MESH,
                 )
+    for k in (5, 6, 7, 8, 9, 0, 1, 2, 3, 4, 10, 11, 12):
+        fetch(k).start()
     pl.semaphore_wait(barrier, ndp * ntp - 1)
+    for k in (5, 6, 7, 8, 9, 10, 11, 12):
+        fetch(k).wait()
 
     sent = []
 
@@ -423,13 +445,35 @@
     def g_side():
         return send(gsend.at[1 - y], grecv, gy_s, gy_r, (other_y, t))
 
-    def g_line(off):
-        zt = (z + off) % nz
-        return send(gzsend.at[zt], gzrecv.at[z], gz_s, gz_r, (2 * zt + y, t))
-
-    def g_lines():
-        whole = gzrecv.at[pl.ds(0, nz - 1)]
-        return send(whole, whole, gz_s, gz_r, (other_y, t))
+    def g_own(i):
+        return gown[y, i] + grecv[i].astype(F32)
+
+    def g_up(zz):
+        part = pl.ds(zz + 1, nz - 1 - zz)
+        return send(gus.at[part], gur.at[part], gu_s, gu_r, (2 * (zz + 1) + y, t))
+
+    def g_down(zz):
+        part = pl.ds(0, zz)
+        return send(gds.at[part], gdr.at[part], gd_s, gd_r, (2 * (zz - 1) + y, t))
+
+    def g_step(ph):
+        @pl.when(z == ph)
+        def _():
+            if ph:
+                g_up(ph - 1).wait_recv()
+            for i in range(ph + 1, nz):
+                gus[i] = (g_own(i) + gur[i].astype(F32) if ph else g_own(i)).astype(BF16)
+            g_up(ph).start()
+
+        top = nz - 1 - ph
+
+        @pl.when(z == top)
+        def _():
+            if ph:
+                g_down(top + 1).wait_recv()
+            for i in range(top):
+                gds[i] = (g_own(i) + gdr[i].astype(F32) if ph else g_own(i)).astype(BF16)
+            g_down(top).start()
 
     def share(dx, dy, u):
         zz = jnp.where(dx == 1, 1 - x, x)
@@ -709,12 +753,13 @@
     frecv[d] = fsend[d]
     rows_in()
     g_side().wait_recv()
-    for i in range(nz):
-        gzsend[i] = (gown[y, i] + grecv[i].astype(F32)).astype(BF16)
+    g_step(0)
     pump(2)
     rows_ready()
     for u in range(len(cuts)):
         unit(lead, u)
+        if 0 < u < nz - 1:
+            g_step(u)
         pump(2)
     dp_wait(2, frecv)
     for i in range(ndp):
@@ -727,8 +772,6 @@
     unit(trail, 0)
     pump(ticks)
     unit(trail, 1)
-    for off in range(1, nz):
-        g_line(off).start()
     for u in range(2, len(cuts)):
         unit(trail, u)
     for u in range(len(cuts)):
@@ -741,10 +784,17 @@
         for dy in range(2):
             emit(dy, u).start()
 
-    g = gown[y, z] + grecv[z].astype(F32)
-    g_lines().wait_recv()
-    for off in range(1, nz):
-        g = g + gzrecv[(z + nz - off) % nz].astype(F32)
+    @pl.when(z == 0)
+    def _():
+        g_down(1).wait_recv()
+        gur[0] = jnp.zeros_like(gur[0])
+
+    @pl.when(z == nz - 1)
+    def _():
+        g_up(nz - 2).wait_recv()
+        gdr[nz - 1] = jnp.zeros_like(gdr[0])
+
+    g = g_own(z) + gur[z].astype(F32) + gdr[z].astype(F32)
     ga_ref[...] = g[0]
     gb_ref[...] = g[1]
     final(1).start()
@@ -789,7 +839,15 @@
     lb_core().wait_send()
     lb_chip().wait_send()
     ab_side(y).wait_send()
-    g_lines().wait_send()
+    for zz in range(nz):
+
+        @pl.when(z == zz)
+        def _():
+            if zz < nz - 1:
+                g_up(zz).wait_send()
+            if zz:
+                g_down(zz).wait_send()
+
 
     @pl.when(t == src_t)
     def _():
@@ -832,7 +890,6 @@
     feats = output_weight_frozen.shape[1]
     chunks = width // CHUNK
     vm = pl.BlockSpec(memory_space=pltpu.VMEM)
-    sm = pl.BlockSpec(memory_space=pltpu.SMEM)
     hbm = pl.BlockSpec(memory_space=pltpu.HBM)
     dma = pltpu.SemaphoreType.DMA
     V = pltpu.VMEM
@@ -844,7 +901,7 @@
             pltpu.VMEM((rank, piece), F32),
             pltpu.VMEM((rank, piece), F32),
         ),
-        in_specs=[vm, vm, hbm, hbm, sm, hbm, vm, vm, hbm, hbm, sm, sm, sm],
+        in_specs=[hbm] * 13,
         out_specs=(pl.BlockSpec(memory_space=pl.ANY),) * 4,
         scratch_shapes=[
             V((ndp, rolls, width), BF16),
@@ -871,6 +928,8 @@
             V((ndp // 2, 2, rank, piece), BF16),
             V((ndp // 2, 2, rank, piece), BF16),
             V((ndp // 2, 2, rank, piece), BF16),
+            V((ndp // 2, 2, rank, piece), BF16),
+            V((ndp // 2, 2, rank, piece), BF16),
             V((rows, shard), BF16),
             V((2, 2, rows, shard), BF16),
             V((2, 2, chunks, feats, CHUNK), BF16),
@@ -892,6 +951,8 @@
             dma,
             dma,
             dma,
+            dma,
+            dma,
             dma((3,)),
             dma((3,)),
             dma((2,)),
@@ -901,7 +962,7 @@
             V((width, qkvw), BF16),
             V((rolls, slots, 2 * HD), BF16),
             V((rows, shard), BF16),
-            dma((5,)),
+            dma((13,)),
             V((rows, shard), F32),
             V((rolls, model), F32),
             V((rank, piece), F32),
@@ -910,7 +971,10 @@
             dma((3,)),
             V((2, rows, 128), F32),
         ]
-        + [dma((2,))] * 8,
+        + [dma((2,))] * 8
+        + [V((rolls, model), BF16), V((model // 128, 128), BF16)]
+        + [V((rank, piece), BF16)] * 2
+        + [pltpu.SMEM((rolls,), t) for t in (jnp.int32, F32, jnp.int32, jnp.int32)],
         compiler_params=pltpu.CompilerParams(
             collective_id=0, has_side_effects=True, vmem_limit_bytes=64815104
         ),

time: 90.3 us -> 88.9 us (0.984)
  Pallas kernels: 89.5 us -> 88.1 us
    pallas_call x1, Pallas kernels: 88.1 us -> 86.7 us  [fused_shards(): pl.pallas_call(lambda *refs: fused_kernel(ndp, ntp, *refs), out_shape=(pl...]
where the time goes in v7:
time: 88.9 us; the launch traced here: 88.8 us
  Pallas kernels  88.1 us (99%)
    pallas_call x1, Pallas kernels, fused_shards(): pl.pallas_call(lambda *refs: fused_kernel(ndp, ntp, *refs), out_shape=(pl...  86.7 us

profile of v7, /device:TPU:3, one launch (start us, length us, event | category | flops | bytes accessed | tf_op | source)
XLA Modules:
  0.0 88.8 jit_solution(16957331454077021934)
XLA Ops:
  0.6 86.7 %shard_map.156 = (f32[2,4096]{1,0:T(2,128)S(1)}, f32[512,1024]{1,0:T(8,128)S(1)}, f32[64,128]{1,0:T(8,128)S(1)}, f32[64,128]{1,0:T(8,128)S(1)}) custom-call(bf16[2,4096]{1,0:T(2,128)(2,1)} %refs_0_.1, bf16[32,128]{1,0:T(8,128)(2,1)} %bitcast.15, bf16[512,1280]{1,0:T(8,128)(2,1)} %bitcast.11, bf16[2,2048,256]{2,1,0:T(8,128)(2,1)} %bitcast.10, s32[2]{0:T(128)} %refs_4_.1, ...), custom_call_target="tpu_custom_call" | custom-call | tf_op jit(solution)/shard_map/pallas_call | solution.py:896
  87.4 1.4 %shard_map.157 = (f32[2,4096]{1,0:T(2,128)}, f32[512,1024]{1,0:T(8,128)}, f32[64,1,128]{2,1,0:T(1,128)}, f32[64,1,128]{2,1,0:T(1,128)}) custom-call(f32[2,4096]{1,0:T(2,128)S(1)} %get-tuple-element.8.refs_0_, f32[512,1024]{1,0:T(8,128)S(1)} %get-tuple-element.9.refs_1_, f32[64,1,128]{2,1,0:T(1,128)S(1)} %bitcast.8, f32[64,1,128]{2,1,0:T(1,128)S(1)} %bitcast.9), custom_call_target="tpu_custom_call" | custom-call | tf_op jit(solution)/shard_map/pallas_call | solution.py:998

commit v8 on v7

--- a/solution.py
+++ b/solution.py
@@ -93,10 +93,10 @@
     rew_in,
     idx_in,
     live_in,
-    dec_out,
-    rows_out,
-    ga_out,
-    gb_out,
+    dec_ref,
+    out_ref,
+    ga_ref,
+    gb_ref,
     hsend,
     stats_ref,
     hbuf,
@@ -117,7 +117,6 @@
     lbhalf,
     lbfull,
     gown,
-    gsend,
     grecv,
     gus,
     gur,
@@ -156,12 +155,6 @@
     cache_ref,
     up_ref,
     in_s,
-    out_ref,
-    dec_ref,
-    ga_ref,
-    gb_ref,
-    out_s,
-    fin_s,
     acc,
     qy_s,
     qy_r,
@@ -443,10 +436,10 @@
         return send(lbfull.at[core], lbfull.at[core], lb_s.at[2], lb_r.at[2], (d, mate))
 
     def g_side():
-        return send(gsend.at[1 - y], grecv, gy_s, gy_r, (other_y, t))
+        return send(gown.at[1 - y], grecv, gy_s, gy_r, (other_y, t))
 
     def g_own(i):
-        return gown[y, i] + grecv[i].astype(F32)
+        return gown[y, i] + grecv[i]
 
     def g_up(zz):
         part = pl.ds(zz + 1, nz - 1 - zz)
@@ -499,14 +492,6 @@
     def columns(yy, u):
         ch, off, num = cuts[u]
         return pl.ds(pl.multiple_of((yy * chunks + ch) * CHUNK + off, 128), num)
-
-    def final(k):
-        src, dst = ((dec_ref, dec_out), (ga_ref, ga_out), (gb_ref, gb_out))[k]
-        return pltpu.make_async_copy(src, dst, fin_s.at[k])
-
-    def emit(dy, u):
-        cols = columns((y + dy) % 2, u)
-        return pltpu.make_async_copy(out_ref.at[:, cols], rows_out.at[:, cols], out_s)
 
     def unit(blk, u):
         ch, off, num = cuts[u]
@@ -704,15 +689,14 @@
             gb = adapter_scale * jnp.dot(low_t, wt_ref[...], preferred_element_type=F32)
             for i in range(ndp):
                 for k, g in enumerate((ga, gb)):
-                    part = g[:, i * piece : (i + 1) * piece]
-                    gown[i % 2, i // 2, k] = part
-                    gsend[i % 2, i // 2, k] = part.astype(BF16)
-            g_side().start()
+                    gown[i % 2, i // 2, k] = g[:, i * piece : (i + 1) * piece]
             out_ref[...] = adapter_scale * lax.dot_general(
                 low_t, bt, TN, preferred_element_type=F32
             )
         a_lines(step).wait_recv()
         a_side(step, y).start()
+        if step == 1:
+            g_side().start()
         pump(1)
         a_side(step, 1 - y).wait_recv()
         attended = jnp.concatenate(
@@ -764,7 +748,6 @@
     dp_wait(2, frecv)
     for i in range(ndp):
         dec_ref[:, i * width : (i + 1) * width] = frecv[i]
-    final(0).start()
     for cp in sent:
         cp.wait_send()
     while clock[0] < 2 * pieces + pieces // 2:
@@ -781,8 +764,6 @@
         for dx, dy in ((1, 0), (0, 1), (1, 1)):
             got = prcv[2 * dx + dy, ch, :, pl.ds(off, num)].astype(F32)
             out_ref[:, columns((y + dy) % 2, u)] += got
-        for dy in range(2):
-            emit(dy, u).start()
 
     @pl.when(z == 0)
     def _():
@@ -797,11 +778,6 @@
     g = g_own(z) + gur[z].astype(F32) + gdr[z].astype(F32)
     ga_ref[...] = g[0]
     gb_ref[...] = g[1]
-    final(1).start()
-    final(2).start()
-    pltpu.make_async_copy(out_ref, rows_out, out_s).wait()
-    for k in range(3):
-        final(k).wait()
 
     def drain(which, full):
         send(full, full, wl_s.at[which], wl_r.at[0, 0, 0], (d, mate)).wait_send()
@@ -902,7 +878,7 @@
             pltpu.VMEM((rank, piece), F32),
         ),
         in_specs=[hbm] * 13,
-        out_specs=(pl.BlockSpec(memory_space=pl.ANY),) * 4,
+        out_specs=(vm,) * 4,
         scratch_shapes=[
             V((ndp, rolls, width), BF16),
             V((2, 128), F32),
@@ -924,8 +900,7 @@
             V((3, 2, rank, rows // 2), F32),
             V((2, 2, rank, rows // 2), BF16),
             V((2, ndp // 2, 2, rank, piece), F32),
-            V((2, ndp // 2, 2, rank, piece), BF16),
-            V((ndp // 2, 2, rank, piece), BF16),
+            V((ndp // 2, 2, rank, piece), F32),
             V((ndp // 2, 2, rank, piece), BF16),
             V((ndp // 2, 2, rank, piece), BF16),
             V((ndp // 2, 2, rank, piece), BF16),
@@ -963,12 +938,6 @@
             V((rolls, slots, 2 * HD), BF16),
             V((rows, shard), BF16),
             dma((13,)),
-            V((rows, shard), F32),
-            V((rolls, model), F32),
-            V((rank, piece), F32),
-            V((rank, piece), F32),
-            dma,
-            dma((3,)),
             V((2, rows, 128), F32),
         ]
         + [dma((2,))] * 8

time: 88.9 us -> 88.7 us (level)
  no operation moved by 1% of the time
where the time goes in v8:
time: 88.7 us; the launch traced here: 88.5 us
  Pallas kernels  87.9 us (99%)
    pallas_call x1, Pallas kernels, fused_shards(): pl.pallas_call(lambda *refs: fused_kernel(ndp, ntp, *refs), out_shape=(pl...  86.5 us

profile of v8, /device:TPU:3, one launch (start us, length us, event | category | flops | bytes accessed | tf_op | source)
XLA Modules:
  0.0 88.5 jit_solution(5946817616515351575)
XLA Ops:
  0.6 86.5 %shard_map.156 = (f32[2,4096]{1,0:T(2,128)S(1)}, f32[512,1024]{1,0:T(8,128)S(1)}, f32[64,128]{1,0:T(8,128)S(1)}, f32[64,128]{1,0:T(8,128)S(1)}) custom-call(bf16[2,4096]{1,0:T(2,128)(2,1)} %refs_0_.1, bf16[32,128]{1,0:T(8,128)(2,1)} %bitcast.15, bf16[512,1280]{1,0:T(8,128)(2,1)} %bitcast.11, bf16[2,2048,256]{2,1,0:T(8,128)(2,1)} %bitcast.10, s32[2]{0:T(128)} %refs_4_.1, ...), custom_call_target="tpu_custom_call" | custom-call | tf_op jit(solution)/shard_map/pallas_call | solution.py:872
  87.2 1.4 %shard_map.157 = (f32[2,4096]{1,0:T(2,128)}, f32[512,1024]{1,0:T(8,128)}, f32[64,1,128]{2,1,0:T(1,128)}, f32[64,1,128]{2,1,0:T(1,128)}) custom-call(f32[2,4096]{1,0:T(2,128)S(1)} %get-tuple-element.8.refs_0_, f32[512,1024]{1,0:T(8,128)S(1)} %get-tuple-element.9.refs_1_, f32[64,1,128]{2,1,0:T(1,128)S(1)} %bitcast.8, f32[64,1,128]{2,1,0:T(1,128)S(1)} %bitcast.9), custom_call_target="tpu_custom_call" | custom-call | tf_op jit(solution)/shard_map/pallas_call | solution.py:967

commit v9 on v8

--- a/solution.py
+++ b/solution.py
@@ -372,7 +372,7 @@
             hop(blk, j, which, zt).start()
 
     clock = [0]
-    ticks = 3 * pieces
+    ticks = 3 * pieces - 2
 
     def tick():
         n = clock[0]
@@ -391,11 +391,11 @@
                 relay_tick("near", near, 2 * m, 2 * m + 2, 3, z_in)
                 relay_tick("far_m", far, 2 * m, 2 * m + 2, 4, z_out)
 
-        if m >= pieces:
+        if m >= pieces - 2:
 
             @pl.when(role_2)
             def _():
-                relay_tick("far_2", far, 2 * (m - pieces), 2 * (m - pieces) + 2, 4, z_out)
+                relay_tick("far_2", far, 2 * (m - pieces + 2), 2 * (m - pieces + 2) + 2, 4, z_out)
 
     def pump(n):
         for _ in range(n):
@@ -750,7 +750,7 @@
         dec_ref[:, i * width : (i + 1) * width] = frecv[i]
     for cp in sent:
         cp.wait_send()
-    while clock[0] < 2 * pieces + pieces // 2:
+    while clock[0] < 2 * pieces + pieces // 2 - 2:
         pump(1)
     unit(trail, 0)
     pump(ticks)

time: 88.7 us -> 88.4 us (level)
  no operation moved by 1% of the time
where the time goes in v9:
time: 88.4 us; the launch traced here: 88.2 us
  Pallas kernels  87.5 us (99%)
    pallas_call x1, Pallas kernels, fused_shards(): pl.pallas_call(lambda *refs: fused_kernel(ndp, ntp, *refs), out_shape=(pl...  86.2 us

profile of v9, /device:TPU:3, one launch (start us, length us, event | category | flops | bytes accessed | tf_op | source)
XLA Modules:
  0.0 88.2 jit_solution(11851932787687944714)
XLA Ops:
  0.6 86.2 %shard_map.156 = (f32[2,4096]{1,0:T(2,128)S(1)}, f32[512,1024]{1,0:T(8,128)S(1)}, f32[64,128]{1,0:T(8,128)S(1)}, f32[64,128]{1,0:T(8,128)S(1)}) custom-call(bf16[2,4096]{1,0:T(2,128)(2,1)} %refs_0_.1, bf16[32,128]{1,0:T(8,128)(2,1)} %bitcast.15, bf16[512,1280]{1,0:T(8,128)(2,1)} %bitcast.11, bf16[2,2048,256]{2,1,0:T(8,128)(2,1)} %bitcast.10, s32[2]{0:T(128)} %refs_4_.1, ...), custom_call_target="tpu_custom_call" | custom-call | tf_op jit(solution)/shard_map/pallas_call | solution.py:872
  86.8 1.4 %shard_map.157 = (f32[2,4096]{1,0:T(2,128)}, f32[512,1024]{1,0:T(8,128)}, f32[64,1,128]{2,1,0:T(1,128)}, f32[64,1,128]{2,1,0:T(1,128)}) custom-call(f32[2,4096]{1,0:T(2,128)S(1)} %get-tuple-element.8.refs_0_, f32[512,1024]{1,0:T(8,128)S(1)} %get-tuple-element.9.refs_1_, f32[64,1,128]{2,1,0:T(1,128)S(1)} %bitcast.8, f32[64,1,128]{2,1,0:T(1,128)S(1)} %bitcast.9), custom_call_target="tpu_custom_call" | custom-call | tf_op jit(solution)/shard_map/pallas_call | solution.py:967
